TPU v7x, 128 devices: a whole 4x4x4 slice. The times are simulated.
128 devices in a mesh: blk: 8 (over z, x_lo), tp: 16 (over x_hi, y, core).
Axes of the slice: x: 4 (x_hi: 2, x_lo: 2; x = x_hi * 2 + x_lo), y: 4, z: 4, core: 2. Of those that a mesh axis runs over, the one named last changes fastest.
Arguments:
- input_pool: bfloat16 [4096, 1792], P(None, 'tp'), may hold values from -6 to 6
- teacher_pool: bfloat16 [4096, 1792], P(None, 'tp'), may hold values from -6 to 6
- gate_weight: bfloat16 [1792, 9472], P(None, 'tp'), may hold values from -0.125 to 0.125
- up_weight: bfloat16 [1792, 9472], P(None, 'tp'), may hold values from -0.125 to 0.125
- params: float32 [8, 9472, 1792], P('blk', 'tp'), may hold values from -6 to 6
- batch_ids: int32 [8, 1024], replicated, may hold values from 0 to 4095
- cycle_order: int32 [8], replicated, may hold values from 0 to 7, each once
- edge_weight: float32 [8], replicated, may hold values from 0.1 to 0.45
Outputs:
- updated: float32 [8, 9472, 1792], P('blk', 'tp')
Inputs may be any that keep to these rules, and one draw needn't show every extreme that they name: `cycle_order`: the 8 cycle positions name 8 different agents.
All inputs are finite; a program needn't handle non-finite values.
Results may differ from a plain program's by a relative error of at most 0.0061.
Values may be sent and summed in bfloat16 or wider, within the bound.
No kernel may reach another device: no remote copies, remote signals or barrier semaphores. Data moves between devices by JAX's collectives and lax.ppermute only.
A program may use at most 128 MiB of HBM per device.

v0:
```python
import jax
import jax.numpy as jnp
from jax import lax
from jax.experimental import pallas as pl
from jax.experimental.pallas import tpu as pltpu
from jax.sharding import PartitionSpec as P


NX, NY, NC = 2, 4, 2
BF = jnp.bfloat16
F32 = jnp.float32
barrier = lax.optimization_barrier


def tp_shift(dx, dy, dc):
    pairs = []
    for x in range(NX):
        for y in range(NY):
            for c in range(NC):
                to = ((x + dx) % NX * NY + (y + dy) % NY) * NC + (c + dc) % NC
                pairs.append(((x * NY + y) * NC + c, to))
    return pairs


def send(array, dx, dy, dc):
    return lax.ppermute(array, "tp", tp_shift(dx, dy, dc))


def hidden_kernel(feature_ref, token_ref, plane_ref, other_ref, gate_ref, up_ref, h_ref, ht_ref, x_ref):
    i = pl.program_id(0)
    blocks = NX * NY
    rows = plane_ref.shape[0] // blocks
    lanes = plane_ref.shape[1] // (NY * NC)
    per = h_ref.shape[0] // lanes
    for j in range(2 * blocks):
        source = plane_ref if j < blocks else other_ref
        at = pl.multiple_of(feature_ref[j] * rows, 16)
        for s in range(per):
            token = pl.multiple_of(token_ref[i * per + s] * lanes, 128)
            x_ref[pl.ds(at, rows), s * lanes : (s + 1) * lanes] = source[
                (j % blocks) * rows : (j % blocks + 1) * rows, pl.ds(token, lanes)
            ]
    x = x_ref[...]
    gate = jnp.dot(gate_ref[...], x, preferred_element_type=F32)
    up = jnp.dot(up_ref[...], x, preferred_element_type=F32)
    hidden = gate / (1.0 + jnp.exp(-gate)) * up
    ht_ref[...] = hidden.astype(BF)
    h_ref[...] = hidden.T.astype(BF)


def make_hidden(feature_order, token_order, plane, other, gate_t, up_t):
    units, features = gate_t.shape
    tokens = plane.shape[1]
    tile = 256
    whole = lambda i, f, t: (0, 0)
    return pl.pallas_call(
        hidden_kernel,
        out_shape=(
            jax.ShapeDtypeStruct((tokens, units), BF),
            jax.ShapeDtypeStruct((units, tokens), BF),
        ),
        grid_spec=pltpu.PrefetchScalarGridSpec(
            num_scalar_prefetch=2,
            grid=(tokens // tile,),
            in_specs=[
                pl.BlockSpec(plane.shape, whole),
                pl.BlockSpec(other.shape, whole),
                pl.BlockSpec(gate_t.shape, whole),
                pl.BlockSpec(up_t.shape, whole),
            ],
            out_specs=[
                pl.BlockSpec((tile, units), lambda i, f, t: (i, 0)),
                pl.BlockSpec((units, tile), lambda i, f, t: (0, i)),
            ],
            scratch_shapes=[pltpu.VMEM((features, tile), BF)],
        ),
        cost_estimate=pl.CostEstimate(
            flops=4 * units * features * tokens,
            transcendentals=units * tokens,
            bytes_accessed=2 * (2 * units * features + features * tokens + 2 * units * tokens),
        ),
        name="make_hidden",
    )(feature_order, token_order, plane, other, gate_t, up_t)


def total(*terms):
    out = terms[0].astype(F32)
    for term in terms[1:]:
        out = out + term.astype(F32)
    return out


def sum_over_units(partial):
    half = partial.shape[0] // NC
    quarter = half // NY
    got = send(partial[half:], 0, 0, 1)
    rest = total(partial[quarter:half], got[quarter:]).astype(BF)
    parts = [send(rest[(d - 1) * quarter : d * quarter], 0, d, 0) for d in (1, 3, 2)]
    mine = total(partial[:quarter], got[:quarter], *parts)
    mine_half = mine.astype(BF)
    mine = total(mine, send(mine_half, 1, 0, 0)).astype(BF)
    back = [send(mine, 0, -d, 0) for d in (1, 3, 2)]
    plane = jnp.concatenate([mine, back[0], back[2], back[1]], axis=0)
    return jnp.concatenate([plane, send(plane, 0, 0, 1)], axis=0)


def body(
    input_pool, teacher_pool, gate_weight, up_weight, params, batch_ids, cycle_order, edge_weight
):
    step = 2.0
    groups = lax.axis_size("tp")
    agents = cycle_order.shape[0]
    place = lax.axis_index("blk")
    at = lax.axis_index("tp")
    core, y, xh = at % NC, (at // NC) % NY, at // (NC * NY)
    slots = jnp.arange(agents, dtype=jnp.int32)

    def edge(offset):
        return jnp.sum(jnp.where(slots == (place + offset) % agents, edge_weight, 0.0))

    weight_next, weight_prev = edge(0), edge(agents - 1)
    weight_self = 1.0 - weight_next - weight_prev
    odd = place % 2 == 1
    coef_own = jnp.where(odd, weight_prev, weight_next)
    coef_got = jnp.where(odd, edge(agents - 2), edge(1))
    agent = jnp.sum(jnp.where(slots == place, cycle_order, 0))
    batch = lax.dynamic_slice_in_dim(batch_ids, agent, 1, 0)[0]

    order = jnp.arange(groups, dtype=jnp.int32)
    dc, dy, dx = order // (NY * NX), (order // NX) % NY, order % NX
    feature_order = ((xh + dx) % NX * NY + (y + dy) % NY) * NC + (core + dc) % NC
    order = jnp.arange(NC * NY, dtype=jnp.int32)
    token_order = (core + order // NY) % NC * NY + (y + order % NY) % NY

    hidden_dev, features = gate_weight.shape[1], gate_weight.shape[0]
    cut = (hidden_dev // 2 + 15) // 16 * 16
    pieces = [slice(0, cut), slice(cut, hidden_dev)]
    zmove = [(i, (i + 2) % agents if i % 2 else (i - 2) % agents) for i in range(agents)]
    xmove = [(i, i ^ 1) for i in range(agents)]

    def along_z(half):
        out = []
        for s in pieces:
            out.append(lax.ppermute(half[s], "blk", zmove))
        return out

    def along_x(half, got, i):
        both = total(coef_own * half[pieces[i]].astype(F32), coef_got * got.astype(F32)).astype(BF)
        return lax.ppermute(both, "blk", xmove)

    rows = jnp.take(input_pool, batch, axis=0).T
    rows, field = barrier((rows, params[0]))
    field_half = field.astype(BF)
    partner = send(rows, 1, 0, 0)
    got = along_z(field_half)
    partner, batch = barrier((partner, batch))
    pair = jnp.concatenate([rows, partner], axis=0)
    parts = [send(pair, 0, -d, 0) for d in (1, 3, 2)]

    batch_rel = jnp.take(batch.reshape(NC * NY, -1), token_order, axis=0).reshape(-1)
    teacher = jnp.take(teacher_pool, batch_rel, axis=0)
    width = teacher.shape[1]
    place_in = (
        lax.broadcasted_iota(jnp.int32, (width, features), 0) + at * width
        == lax.broadcasted_iota(jnp.int32, (width, features), 1)
    ).astype(BF)
    teacher_wide = jnp.dot(teacher, place_in, preferred_element_type=F32).astype(BF)

    parts, teacher_wide = barrier((parts, teacher_wide))
    plane = jnp.concatenate([pair, parts[0], parts[2], parts[1]], axis=0)
    plane, got[0] = barrier((plane, got[0]))
    other = send(plane, 0, 0, 1)
    side = [along_x(field_half, got[0], 0)]
    hidden, hidden_t = make_hidden(
        feature_order, token_order, plane, other, gate_weight.T, up_weight.T
    )
    hidden, got[1] = barrier((hidden, got[1]))
    side.append(along_x(field_half, got[1], 1))
    scale = float(hidden_dev * groups) ** (-0.5)

    def partial_out(half):
        out = scale * jnp.dot(hidden, half, preferred_element_type=F32)
        return (out - teacher_wide.astype(F32)).astype(BF)

    def gradient(resid):
        return scale * jnp.dot(hidden_t, resid, preferred_element_type=F32)

    resid = sum_over_units(partial_out(field_half))
    mixed = weight_self * field + jnp.concatenate(side, axis=0).astype(F32)
    first = gradient(resid)
    combined = mixed - (2.0 * step) * first
    combined_half = combined.astype(BF)
    got = along_z(combined_half)
    moved = (mixed - step * first).astype(BF)
    base = weight_self * combined + step * first
    side = [along_x(combined_half, g, i) for i, g in enumerate(got)]
    second = gradient(sum_over_units(partial_out(moved)))
    return (base + jnp.concatenate(side, axis=0).astype(F32) - step * second)[None]


def solution(mesh):
    placed = (
        P(None, "tp"),
        P(None, "tp"),
        P(None, "tp"),
        P(None, "tp"),
        P("blk", "tp", None),
        P(),
        P(),
        P(),
    )

    return jax.shard_map(
        body, mesh=mesh, in_specs=placed, out_specs=P("blk", "tp", None), check_vma=False
    )
```

profile of v0, /device:TPU:0, one launch (start us, length us, event | category | flops | bytes accessed | tf_op | source)
XLA Modules:
  0.0 341.8 jit_solution(8057110977298962373)
XLA Ops:
  0.0 1.3 fusion.22
  3.3 1.6 copy.9
  5.0 3.2 gather_fusion.1
  8.3 3.2 collective-permute-start
  11.6 2.4 convert_element_type.131
  14.0 1.1 slice.90
  15.0 4.0 %collective-permute-start.4 = (bf16[304,1792]{1,0:T(8,128)(2,1)}, bf16[304,1792]{1,0:T(8,128)(2,1)}, u32[]{:S(2)}, u32[]{:S(2)}) collective-permute-start(bf16[304,1792]{1,0:T(8,128)(2,1)} %slice.90), channel_id=1, source_target_pairs={{0,96},{16,48},{32,0},{48,80},{64,32},{80,112},{96,64},{112,16},{1... | collective-permute-start | bytes 3268616 | tf_op jit(solution)/shard_map/ppermute | solution.py:144
  19.6 1.6 copy.11
  21.3 0.8 constant_dynamic-update-slice_fusion.1
  22.1 1.8 constant_dynamic-update-slice_fusion
  23.9 3.2 collective-permute-start.3
  27.7 2.6 collective-permute-start.1
  30.9 3.2 gather_fusion.2
  34.2 3.0 convolution_convert_fusion
  37.3 1.9 collective-permute-done.3
  39.1 8.1 %collective-permute-done.2 = bf16[224,1024]{1,0:T(8,128)(2,1)} collective-permute-done((bf16[224,1024]{1,0:T(8,128)(2,1)}, bf16[224,1024]{1,0:T(8,128)(2,1)}, u32[]{:S(2)}, u32[]{:S(2)}) %collective-permute-start.2) | collective-permute-done | bytes 458784 | tf_op jit(solution)/shard_map/ppermute | solution.py:26
  47.6 1.8 constant_dynamic-update-slice_fusion.4
  49.4 1.8 constant_dynamic-update-slice_fusion.3
  51.3 1.8 constant_dynamic-update-slice_fusion.2.plane_ref
  53.1 1.0 slice.91
  55.1 2.1 collective-permute-done.6.other_ref
  57.2 11.3 %make_hidden.1 = (bf16[1024,592]{1,0:T(8,128)(2,1)}, bf16[592,1024]{1,0:T(8,128)(2,1)}) custom-call(s32[16]{0:T(128)} %fusion.16.feature_ref, s32[8]{0:T(128)} %get-tuple-element.43.token_ref, bf16[896,1024]{1,0:T(8,128)(2,1)} %constant_dynamic-update-slice_fusion.2.plane_ref, bf16[896,1024]{1,0:T(8,128)(2,1)} %collective-permute-done.6.other_ref, ...), custom_call_target="tpu_custom_call" | custom-call | flops 4345298944 | bytes 10338304 | tf_op jit(solution)/shard_map/make_hidden/pallas_call | solution.py:56
  68.6 11.0 %collective-permute-done.7 = bf16[288,1792]{1,0:T(8,128)(2,1)S(1)} collective-permute-done((bf16[288,1792]{1,0:T(8,128)(2,1)}, bf16[288,1792]{1,0:T(8,128)(2,1)S(1)}, u32[]{:S(2)}, u32[]{:S(2)}) %collective-permute-start.7) | collective-permute-done | bytes 1032224 | tf_op jit(solution)/shard_map/ppermute | solution.py:144
  79.6 5.7 %fusion = bf16[1024,1792]{1,0:T(8,128)(2,1)S(1)} fusion(bf16[1024,1792]{1,0:T(8,128)(2,1)} %convolution_convert_fusion, bf16[1024,592]{1,0:T(8,128)(2,1)} %get-tuple-element.32, bf16[592,1792]{1,0:T(8,128)(2,1)S(1)} %convert_element_type.131), kind=kOutput, calls=%fused_computation.5 | convolution fusion | flops 2179989504 | bytes 10674176 | tf_op jit(solution)/shard_map/dot_general | solution.py:182
  85.5 3.8 %collective-permute-done.9 = bf16[512,1792]{1,0:T(8,128)(2,1)S(1)} collective-permute-done((bf16[512,1792]{1,0:T(8,128)(2,1)S(1)}, bf16[512,1792]{1,0:T(8,128)(2,1)S(1)}, u32[]{:S(2)}, u32[]{:S(2)}) %collective-permute-start.9) | collective-permute-done | bytes 1835040 | tf_op jit(solution)/shard_map/ppermute | solution.py:26
  89.8 1.4 collective-permute-start.10
  91.2 2.7 collective-permute-start.12
  94.5 9.1 %collective-permute-done.10 = bf16[128,1792]{1,0:T(8,128)(2,1)S(1)} collective-permute-done((bf16[128,1792]{1,0:T(8,128)(2,1)S(1)}, bf16[128,1792]{1,0:T(8,128)(2,1)S(1)}, u32[]{:S(2)}, u32[]{:S(2)}) %collective-permute-start.10) | collective-permute-done | bytes 458784 | tf_op jit(solution)/shard_map/ppermute | solution.py:26
  103.6 10.7 %collective-permute-done.12 = bf16[128,1792]{1,0:T(8,128)(2,1)S(1)} collective-permute-done((bf16[128,1792]{1,0:T(8,128)(2,1)S(1)}, bf16[128,1792]{1,0:T(8,128)(2,1)S(1)}, u32[]{:S(2)}, u32[]{:S(2)}) %collective-permute-start.12) | collective-permute-done | bytes 458784 | tf_op jit(solution)/shard_map/ppermute | solution.py:26
  115.2 12.7 %collective-permute-done.13 = bf16[128,1792]{1,0:T(8,128)(2,1)S(1)} collective-permute-done((bf16[128,1792]{1,0:T(8,128)(2,1)S(1)}, bf16[128,1792]{1,0:T(8,128)(2,1)S(1)}, u32[]{:S(2)}, u32[]{:S(2)}) %collective-permute-start.13) | collective-permute-done | bytes 458784 | tf_op jit(solution)/shard_map/ppermute | solution.py:26
  127.9 1.3 constant_dynamic-update-slice_fusion.11
  129.2 1.9 collective-permute-start.16
  131.1 2.7 collective-permute-start.15
  136.9 6.1 %collective-permute-done.16 = bf16[128,1792]{1,0:T(8,128)(2,1)S(1)} collective-permute-done((bf16[128,1792]{1,0:T(8,128)(2,1)}, bf16[128,1792]{1,0:T(8,128)(2,1)S(1)}, u32[]{:S(2)}, u32[]{:S(2)}) %collective-permute-start.16) | collective-permute-done | bytes 458784 | tf_op jit(solution)/shard_map/ppermute | solution.py:26
  143.0 10.4 %collective-permute-done.15 = bf16[128,1792]{1,0:T(8,128)(2,1)S(1)} collective-permute-done((bf16[128,1792]{1,0:T(8,128)(2,1)}, bf16[128,1792]{1,0:T(8,128)(2,1)S(1)}, u32[]{:S(2)}, u32[]{:S(2)}) %collective-permute-start.15) | collective-permute-done | bytes 458784 | tf_op jit(solution)/shard_map/ppermute | solution.py:26
  153.4 2.4 pad_maximum_fusion.1
  155.8 2.7 add_convert_fusion.3
  158.6 1.4 add_convert_fusion.5
  160.0 2.0 collective-permute-start.8
  163.3 0.8 constant_dynamic-update-slice_fusion.10
  164.1 0.8 constant_dynamic-update-slice_fusion.9
  164.9 0.8 constant_dynamic-update-slice_fusion.8
  165.7 3.0 constant_dynamic-update-slice_fusion.7
  168.7 17.1 %collective-permute-done.5 = bf16[304,1792]{1,0:T(8,128)(2,1)} collective-permute-done((bf16[304,1792]{1,0:T(8,128)(2,1)}, bf16[304,1792]{1,0:T(8,128)(2,1)}, u32[]{:S(2)}, u32[]{:S(2)}) %collective-permute-start.5) | collective-permute-done | bytes 1089568 | tf_op jit(solution)/shard_map/ppermute | solution.py:149
  185.8 21.5 %collective-permute-done.8 = bf16[288,1792]{1,0:T(8,128)(2,1)S(1)} collective-permute-done((bf16[288,1792]{1,0:T(8,128)(2,1)}, bf16[288,1792]{1,0:T(8,128)(2,1)S(1)}, u32[]{:S(2)}, u32[]{:S(2)}) %collective-permute-start.8) | collective-permute-done | bytes 1032224 | tf_op jit(solution)/shard_map/ppermute | solution.py:149
  207.2 1.0 copy-done.6
  208.2 6.4 %fusion.2 = (bf16[592,1792]{1,0:T(8,128)(2,1)S(1)}, f32[592,1792]{1,0:T(8,128)S(1)}) fusion(f32[592,1792]{1,0:T(8,128)} %bitcast.25, f32[]{:T(128)S(6)} %sub.42, bf16[288,1792]{1,0:T(8,128)(2,1)} %copy-done.6, bf16[304,1792]{1,0:T(8,128)(2,1)} %collective-permute-done.5, bf16[592,1024]{1,0:T(8,128)(2,1)S(1)} %copy-done.9, ...), kind=kOutput, calls=%fused_computation.16 | convolution fusion | flops 2182197248 | bytes 17612804 | tf_op jit(solution)/shard_map/dot_general | solution.py:186
  214.7 4.4 %fusion.1 = bf16[1024,1792]{1,0:T(8,128)(2,1)S(1)} fusion(bf16[1024,1792]{1,0:T(8,128)(2,1)S(1)} %copy-done.2, bf16[1024,592]{1,0:T(8,128)(2,1)S(1)} %copy-done.8, f32[592,1792]{1,0:T(8,128)S(1)} %get-tuple-element.55, f32[592,1792]{1,0:T(8,128)S(1)} %bitcast.28, f32[]{:T(128)S(6)} %sub.42, bf16[288,1792]{1,0:T(8,128)(2,1)S(1)} %copy-done.7, ...), kind=kOutput, calls=%fused_computation.6 | convolution fusion | flops 2189537280 | bytes 19161092 | tf_op jit(solution)/shard_map/dot_general | solution.py:182
  219.4 3.8 %collective-permute-done.22 = bf16[512,1792]{1,0:T(8,128)(2,1)S(1)} collective-permute-done((bf16[512,1792]{1,0:T(8,128)(2,1)S(1)}, bf16[512,1792]{1,0:T(8,128)(2,1)S(1)}, u32[]{:S(2)}, u32[]{:S(2)}) %collective-permute-start.22) | collective-permute-done | bytes 1835040 | tf_op jit(solution)/shard_map/ppermute | solution.py:26
  223.6 0.9 collective-permute-start.23
  224.5 2.7 collective-permute-start.25
  227.8 10.2 %collective-permute-done.23 = bf16[128,1792]{1,0:T(8,128)(2,1)S(1)} collective-permute-done((bf16[128,1792]{1,0:T(8,128)(2,1)S(1)}, bf16[128,1792]{1,0:T(8,128)(2,1)S(1)}, u32[]{:S(2)}, u32[]{:S(2)}) %collective-permute-start.23) | collective-permute-done | bytes 458784 | tf_op jit(solution)/shard_map/ppermute | solution.py:26
  238.0 9.6 %collective-permute-done.25 = bf16[128,1792]{1,0:T(8,128)(2,1)S(1)} collective-permute-done((bf16[128,1792]{1,0:T(8,128)(2,1)S(1)}, bf16[128,1792]{1,0:T(8,128)(2,1)S(1)}, u32[]{:S(2)}, u32[]{:S(2)}) %collective-permute-start.25) | collective-permute-done | bytes 458784 | tf_op jit(solution)/shard_map/ppermute | solution.py:26
  248.9 2.9 collective-permute-start.18
  251.8 9.4 %collective-permute-done.26 = bf16[128,1792]{1,0:T(8,128)(2,1)S(1)} collective-permute-done((bf16[128,1792]{1,0:T(8,128)(2,1)S(1)}, bf16[128,1792]{1,0:T(8,128)(2,1)S(1)}, u32[]{:S(2)}, u32[]{:S(2)}) %collective-permute-start.26) | collective-permute-done | bytes 458784 | tf_op jit(solution)/shard_map/ppermute | solution.py:26
  261.6 1.9 collective-permute-start.29
  263.6 3.2 collective-permute-start.28
  266.9 1.7 collective-permute-start.20
  268.6 7.3 %collective-permute-done.29 = bf16[128,1792]{1,0:T(8,128)(2,1)S(1)} collective-permute-done((bf16[128,1792]{1,0:T(8,128)(2,1)S(1)}, bf16[128,1792]{1,0:T(8,128)(2,1)S(1)}, u32[]{:S(2)}, u32[]{:S(2)}) %collective-permute-start.29) | collective-permute-done | bytes 458784 | tf_op jit(solution)/shard_map/ppermute | solution.py:26
  275.8 10.4 %collective-permute-done.28 = bf16[128,1792]{1,0:T(8,128)(2,1)S(1)} collective-permute-done((bf16[128,1792]{1,0:T(8,128)(2,1)S(1)}, bf16[128,1792]{1,0:T(8,128)(2,1)S(1)}, u32[]{:S(2)}, u32[]{:S(2)}) %collective-permute-start.28) | collective-permute-done | bytes 458784 | tf_op jit(solution)/shard_map/ppermute | solution.py:26
  287.4 8.7 %collective-permute-done.20 = bf16[288,1792]{1,0:T(8,128)(2,1)S(1)} collective-permute-done((bf16[288,1792]{1,0:T(8,128)(2,1)S(1)}, bf16[288,1792]{1,0:T(8,128)(2,1)S(1)}, u32[]{:S(2)}, u32[]{:S(2)}) %collective-permute-start.20) | collective-permute-done | bytes 1032224 | tf_op jit(solution)/shard_map/ppermute | solution.py:144
  296.5 1.5 collective-permute-start.21
  298.2 37.5 %collective-permute-done.21 = bf16[288,1792]{1,0:T(8,128)(2,1)S(1)} collective-permute-done((bf16[288,1792]{1,0:T(8,128)(2,1)S(1)}, bf16[288,1792]{1,0:T(8,128)(2,1)S(1)}, u32[]{:S(2)}, u32[]{:S(2)}) %collective-permute-start.21) | collective-permute-done | bytes 1032224 | tf_op jit(solution)/shard_map/ppermute | solution.py:149
  335.7 6.1 %subtract_bitcast_fusion = f32[1,592,1792]{2,1,0:T(8,128)} fusion(f32[592,1792]{1,0:T(8,128)S(1)} %get-tuple-element.55, bf16[592,1024]{1,0:T(8,128)(2,1)S(1)} %copy-done.9, bf16[1024,1792]{1,0:T(8,128)(2,1)S(1)} %constant_dynamic-update-slice_fusion.12, f32[592,1792]{1,0:T(8,128)S(1)} %bitcast.29, bf16[288,1792]{1,0:T(8,128)(2,1)S(1)} %collective-permute-done.21, ...), kind=kOutput, calls=%fused_computation.7 | convolution fusion | flops 2191745024 | bytes 21856260 | tf_op jit(solution)/shard_map/dot_general | solution.py:186
  (81 shorter events, 11.3 us)
Async XLA Ops:
  0.0 3.2 copy-start
  8.3 13.8 %collective-permute-start = (bf16[112,1024]{1,0:T(8,128)(2,1)S(1)}, bf16[112,1024]{1,0:T(8,128)(2,1)}, u32[]{:S(2)}, u32[]{:S(2)}) collective-permute-start(bf16[112,1024]{1,0:T(8,128)(2,1)S(1)} %select_bitcast_fusion), channel_id=1, source_target_pairs={{0,8},{1,9},{2,10},{3,11},{4,12},{5,13},{6,14},{7,15},{8,0},{9,1},... | collective-permute-start | bytes 688136 | tf_op jit(solution)/shard_map/ppermute | solution.py:26
  15.0 38.0 %collective-permute-start.4 = (bf16[304,1792]{1,0:T(8,128)(2,1)}, bf16[304,1792]{1,0:T(8,128)(2,1)}, u32[]{:S(2)}, u32[]{:S(2)}) collective-permute-start(bf16[304,1792]{1,0:T(8,128)(2,1)} %slice.90), channel_id=1, source_target_pairs={{0,96},{16,48},{32,0},{48,80},{64,32},{80,112},{96,64},{112,16},{1... | collective-permute-start | bytes 3268616 | tf_op jit(solution)/shard_map/ppermute | solution.py:144
  23.9 15.3 %collective-permute-start.3 = (bf16[224,1024]{1,0:T(8,128)(2,1)}, bf16[224,1024]{1,0:T(8,128)(2,1)}, u32[]{:S(2)}, u32[]{:S(2)}) collective-permute-start(bf16[224,1024]{1,0:T(8,128)(2,1)} %get-tuple-element.50), channel_id=1, source_target_pairs={{0,4},{1,5},{2,6},{3,7},{4,0},{5,1},{6,2},{7,3},{8,12},{9,13},{10,... | collective-permute-start | bytes 1376264 | tf_op jit(solution)/shard_map/ppermute | solution.py:26
  27.1 20.2 %collective-permute-start.2 = (bf16[224,1024]{1,0:T(8,128)(2,1)}, bf16[224,1024]{1,0:T(8,128)(2,1)}, u32[]{:S(2)}, u32[]{:S(2)}) collective-permute-start(bf16[224,1024]{1,0:T(8,128)(2,1)} %get-tuple-element.50), channel_id=1, source_target_pairs={{0,2},{1,3},{2,4},{3,5},{4,6},{5,7},{6,0},{7,1},{8,10},{9,11},{10,... | collective-permute-start | bytes 1376264 | tf_op jit(solution)/shard_map/ppermute | solution.py:26
  27.7 19.9 %collective-permute-start.1 = (bf16[224,1024]{1,0:T(8,128)(2,1)}, bf16[224,1024]{1,0:T(8,128)(2,1)}, u32[]{:S(2)}, u32[]{:S(2)}) collective-permute-start(bf16[224,1024]{1,0:T(8,128)(2,1)} %get-tuple-element.50), channel_id=1, source_target_pairs={{0,6},{1,7},{2,0},{3,1},{4,2},{5,3},{6,4},{7,5},{8,14},{9,15},{10,... | collective-permute-start | bytes 1376264 | tf_op jit(solution)/shard_map/ppermute | solution.py:26
  53.1 4.1 %collective-permute-start.6 = (bf16[896,1024]{1,0:T(8,128)(2,1)}, bf16[896,1024]{1,0:T(8,128)(2,1)}, u32[]{:S(2)}, u32[]{:S(2)}) collective-permute-start(bf16[896,1024]{1,0:T(8,128)(2,1)} %constant_dynamic-update-slice_fusion.2.plane_ref), channel_id=1, source_target_pairs={{0,1},{1,0},{2,3},{3,2},{4,5},{5,4},{6,7},{7,6},{8,9},{9,8},{10,11... | collective-permute-start | bytes 5505032 | tf_op jit(solution)/shard_map/ppermute | solution.py:26
  54.1 25.4 %collective-permute-start.7 = (bf16[288,1792]{1,0:T(8,128)(2,1)}, bf16[288,1792]{1,0:T(8,128)(2,1)S(1)}, u32[]{:S(2)}, u32[]{:S(2)}) collective-permute-start(bf16[288,1792]{1,0:T(8,128)(2,1)} %slice.91), channel_id=1, source_target_pairs={{0,96},{16,48},{32,0},{48,80},{64,32},{80,112},{96,64},{112,16},{1... | collective-permute-start | bytes 3096584 | tf_op jit(solution)/shard_map/ppermute | solution.py:144
  79.6 5.7 %copy-start.3 = (bf16[288,1792]{1,0:T(8,128)(2,1)}, bf16[288,1792]{1,0:T(8,128)(2,1)S(1)}, u32[]{:S(2)}) copy-start(bf16[288,1792]{1,0:T(8,128)(2,1)S(1)} %collective-permute-done.7) | copy-start | bytes 3096580
  85.4 3.9 %collective-permute-start.9 = (bf16[512,1792]{1,0:T(8,128)(2,1)S(1)}, bf16[512,1792]{1,0:T(8,128)(2,1)S(1)}, u32[]{:S(2)}, u32[]{:S(2)}) collective-permute-start(bf16[512,1792]{1,0:T(8,128)(2,1)S(1)} %slice.93), channel_id=1, source_target_pairs={{0,1},{1,0},{2,3},{3,2},{4,5},{5,4},{6,7},{7,6},{8,9},{9,8},{10,11... | collective-permute-start | bytes 5505032 | tf_op jit(solution)/shard_map/ppermute | solution.py:26
  89.8 13.8 %collective-permute-start.10 = (bf16[128,1792]{1,0:T(8,128)(2,1)S(1)}, bf16[128,1792]{1,0:T(8,128)(2,1)S(1)}, u32[]{:S(2)}, u32[]{:S(2)}) collective-permute-start(bf16[128,1792]{1,0:T(8,128)(2,1)S(1)} %get-tuple-element.47), channel_id=1, source_target_pairs={{0,2},{1,3},{2,4},{3,5},{4,6},{5,7},{6,0},{7,1},{8,10},{9,11},{10,... | collective-permute-start | bytes 1376264 | tf_op jit(solution)/shard_map/ppermute | solution.py:26
  91.2 23.1 %collective-permute-start.12 = (bf16[128,1792]{1,0:T(8,128)(2,1)S(1)}, bf16[128,1792]{1,0:T(8,128)(2,1)S(1)}, u32[]{:S(2)}, u32[]{:S(2)}) collective-permute-start(bf16[128,1792]{1,0:T(8,128)(2,1)S(1)} %get-tuple-element.48), channel_id=1, source_target_pairs={{0,4},{1,5},{2,6},{3,7},{4,0},{5,1},{6,2},{7,3},{8,12},{9,13},{10,... | collective-permute-start | bytes 1376264 | tf_op jit(solution)/shard_map/ppermute | solution.py:26
  93.9 20.4 %collective-permute-start.11 = (bf16[128,1792]{1,0:T(8,128)(2,1)S(1)}, bf16[128,1792]{1,0:T(8,128)(2,1)S(1)}, u32[]{:S(2)}, u32[]{:S(2)}) collective-permute-start(bf16[128,1792]{1,0:T(8,128)(2,1)S(1)} %get-tuple-element.49), channel_id=1, source_target_pairs={{0,6},{1,7},{2,0},{3,1},{4,2},{5,3},{6,4},{7,5},{8,14},{9,15},{10,... | collective-permute-start | bytes 1376264 | tf_op jit(solution)/shard_map/ppermute | solution.py:26
  114.6 19.2 %copy-start.5 = (f32[8]{0:T(128)S(1)}, f32[8]{0:T(128)}, u32[]{:S(2)}) copy-start(f32[8]{0:T(128)} %param.17) | copy-start | bytes 100
  114.6 13.3 %collective-permute-start.13 = (bf16[128,1792]{1,0:T(8,128)(2,1)S(1)}, bf16[128,1792]{1,0:T(8,128)(2,1)S(1)}, u32[]{:S(2)}, u32[]{:S(2)}) collective-permute-start(bf16[128,1792]{1,0:T(8,128)(2,1)S(1)} %fusion.43), channel_id=1, source_target_pairs={{0,8},{1,9},{2,10},{3,11},{4,12},{5,13},{6,14},{7,15},{8,0},{9,1},... | collective-permute-start | bytes 1376264 | tf_op jit(solution)/shard_map/ppermute | solution.py:26
  129.2 13.8 %collective-permute-start.16 = (bf16[128,1792]{1,0:T(8,128)(2,1)}, bf16[128,1792]{1,0:T(8,128)(2,1)S(1)}, u32[]{:S(2)}, u32[]{:S(2)}) collective-permute-start(bf16[128,1792]{1,0:T(8,128)(2,1)} %get-tuple-element.41), channel_id=1, source_target_pairs={{0,2},{1,3},{2,4},{3,5},{4,6},{5,7},{6,0},{7,1},{8,10},{9,11},{10,... | collective-permute-start | bytes 1376264 | tf_op jit(solution)/shard_map/ppermute | solution.py:26
  131.1 22.3 %collective-permute-start.15 = (bf16[128,1792]{1,0:T(8,128)(2,1)}, bf16[128,1792]{1,0:T(8,128)(2,1)S(1)}, u32[]{:S(2)}, u32[]{:S(2)}) collective-permute-start(bf16[128,1792]{1,0:T(8,128)(2,1)} %get-tuple-element.41), channel_id=1, source_target_pairs={{0,4},{1,5},{2,6},{3,7},{4,0},{5,1},{6,2},{7,3},{8,12},{9,13},{10,... | collective-permute-start | bytes 1376264 | tf_op jit(solution)/shard_map/ppermute | solution.py:26
  133.8 19.6 %collective-permute-start.14 = (bf16[128,1792]{1,0:T(8,128)(2,1)}, bf16[128,1792]{1,0:T(8,128)(2,1)S(1)}, u32[]{:S(2)}, u32[]{:S(2)}) collective-permute-start(bf16[128,1792]{1,0:T(8,128)(2,1)} %get-tuple-element.41), channel_id=1, source_target_pairs={{0,6},{1,7},{2,0},{3,1},{4,2},{5,3},{6,4},{7,5},{8,14},{9,15},{10,... | collective-permute-start | bytes 1376264 | tf_op jit(solution)/shard_map/ppermute | solution.py:26
  155.8 2.7 copy-start.4
  155.8 9.9 %collective-permute-start.17 = (bf16[512,1792]{1,0:T(8,128)(2,1)}, bf16[512,1792]{1,0:T(8,128)(2,1)}, u32[]{:S(2)}, u32[]{:S(2)}) collective-permute-start(bf16[512,1792]{1,0:T(8,128)(2,1)} %pad_maximum_fusion.1), channel_id=1, source_target_pairs={{0,1},{1,0},{2,3},{3,2},{4,5},{5,4},{6,7},{7,6},{8,9},{9,8},{10,11... | collective-permute-start | bytes 5505032 | tf_op jit(solution)/shard_map/ppermute | solution.py:26
  158.6 27.2 %collective-permute-start.5 = (bf16[304,1792]{1,0:T(8,128)(2,1)}, bf16[304,1792]{1,0:T(8,128)(2,1)}, u32[]{:S(2)}, u32[]{:S(2)}) collective-permute-start(bf16[304,1792]{1,0:T(8,128)(2,1)} %add_convert_fusion.3), channel_id=1, source_target_pairs={{0,16},{16,0},{32,48},{48,32},{64,80},{80,64},{96,112},{112,96},{1... | collective-permute-start | bytes 3268616 | tf_op jit(solution)/shard_map/ppermute | solution.py:149
  160.0 47.3 %collective-permute-start.8 = (bf16[288,1792]{1,0:T(8,128)(2,1)}, bf16[288,1792]{1,0:T(8,128)(2,1)S(1)}, u32[]{:S(2)}, u32[]{:S(2)}) collective-permute-start(bf16[288,1792]{1,0:T(8,128)(2,1)} %add_convert_fusion.5), channel_id=1, source_target_pairs={{0,16},{16,0},{32,48},{48,32},{64,80},{80,64},{96,112},{112,96},{1... | collective-permute-start | bytes 3096584 | tf_op jit(solution)/shard_map/ppermute | solution.py:149
  164.9 43.3 %copy-start.9 = (bf16[592,1024]{1,0:T(8,128)(2,1)S(1)}, bf16[592,1024]{1,0:T(8,128)(2,1)}, u32[]{:S(2)}) copy-start(bf16[592,1024]{1,0:T(8,128)(2,1)} %get-tuple-element.31) | copy-start | bytes 3637252
  165.7 49.0 %slice-start = ((s8[4243456]{0:T(1024)(128)(4,1)}), s8[4194304]{0:T(1024)(128)(4,1)S(1)}, s32[]{:S(2)}) async-start(s8[4243456]{0:T(1024)(128)(4,1)} %bitcast.26), calls=%async_computation | async-start | bytes 8388608
  207.2 1.0 copy-start.6
  208.2 6.5 %slice-start.1 = ((s8[4243456]{0:T(1024)(128)(4,1)}), s8[49152]{0:T(1024)(128)(4,1)S(1)}, s32[]{:S(2)}) async-start(s8[4243456]{0:T(1024)(128)(4,1)} %bitcast.26), calls=%async_computation.1 | async-start | bytes 98304
  208.2 6.5 %copy-start.2 = (bf16[1024,1792]{1,0:T(8,128)(2,1)S(1)}, bf16[1024,1792]{1,0:T(8,128)(2,1)}, u32[]{:S(2)}) copy-start(bf16[1024,1792]{1,0:T(8,128)(2,1)} %convolution_convert_fusion) | copy-start | bytes 11010052
  208.2 6.5 %copy-start.7 = (bf16[288,1792]{1,0:T(8,128)(2,1)S(1)}, bf16[288,1792]{1,0:T(8,128)(2,1)}, u32[]{:S(2)}) copy-start(bf16[288,1792]{1,0:T(8,128)(2,1)} %copy-done.6) | copy-start | bytes 3096580
  208.2 6.5 %copy-start.8 = (bf16[1024,592]{1,0:T(8,128)(2,1)S(1)}, bf16[1024,592]{1,0:T(8,128)(2,1)}, u32[]{:S(2)}) copy-start(bf16[1024,592]{1,0:T(8,128)(2,1)} %get-tuple-element.32) | copy-start | bytes 3637252
  219.3 3.9 %collective-permute-start.22 = (bf16[512,1792]{1,0:T(8,128)(2,1)S(1)}, bf16[512,1792]{1,0:T(8,128)(2,1)S(1)}, u32[]{:S(2)}, u32[]{:S(2)}) collective-permute-start(bf16[512,1792]{1,0:T(8,128)(2,1)S(1)} %slice.103), channel_id=1, source_target_pairs={{0,1},{1,0},{2,3},{3,2},{4,5},{5,4},{6,7},{7,6},{8,9},{9,8},{10,11... | collective-permute-start | bytes 5505032 | tf_op jit(solution)/shard_map/ppermute | solution.py:26
  223.6 14.4 %collective-permute-start.23 = (bf16[128,1792]{1,0:T(8,128)(2,1)S(1)}, bf16[128,1792]{1,0:T(8,128)(2,1)S(1)}, u32[]{:S(2)}, u32[]{:S(2)}) collective-permute-start(bf16[128,1792]{1,0:T(8,128)(2,1)S(1)} %get-tuple-element.44), channel_id=1, source_target_pairs={{0,2},{1,3},{2,4},{3,5},{4,6},{5,7},{6,0},{7,1},{8,10},{9,11},{10,... | collective-permute-start | bytes 1376264 | tf_op jit(solution)/shard_map/ppermute | solution.py:26
  224.5 23.0 %collective-permute-start.25 = (bf16[128,1792]{1,0:T(8,128)(2,1)S(1)}, bf16[128,1792]{1,0:T(8,128)(2,1)S(1)}, u32[]{:S(2)}, u32[]{:S(2)}) collective-permute-start(bf16[128,1792]{1,0:T(8,128)(2,1)S(1)} %get-tuple-element.45), channel_id=1, source_target_pairs={{0,4},{1,5},{2,6},{3,7},{4,0},{5,1},{6,2},{7,3},{8,12},{9,13},{10,... | collective-permute-start | bytes 1376264 | tf_op jit(solution)/shard_map/ppermute | solution.py:26
  227.2 20.7 %collective-permute-start.24 = (bf16[128,1792]{1,0:T(8,128)(2,1)S(1)}, bf16[128,1792]{1,0:T(8,128)(2,1)S(1)}, u32[]{:S(2)}, u32[]{:S(2)}) collective-permute-start(bf16[128,1792]{1,0:T(8,128)(2,1)S(1)} %get-tuple-element.46), channel_id=1, source_target_pairs={{0,6},{1,7},{2,0},{3,1},{4,2},{5,3},{6,4},{7,5},{8,14},{9,15},{10,... | collective-permute-start | bytes 1376264 | tf_op jit(solution)/shard_map/ppermute | solution.py:26
  248.2 13.0 %collective-permute-start.26 = (bf16[128,1792]{1,0:T(8,128)(2,1)S(1)}, bf16[128,1792]{1,0:T(8,128)(2,1)S(1)}, u32[]{:S(2)}, u32[]{:S(2)}) collective-permute-start(bf16[128,1792]{1,0:T(8,128)(2,1)S(1)} %fusion.44), channel_id=1, source_target_pairs={{0,8},{1,9},{2,10},{3,11},{4,12},{5,13},{6,14},{7,15},{8,0},{9,1},... | collective-permute-start | bytes 1376264 | tf_op jit(solution)/shard_map/ppermute | solution.py:26
  248.9 37.8 %collective-permute-start.18 = (bf16[304,1792]{1,0:T(8,128)(2,1)S(1)}, bf16[304,1792]{1,0:T(8,128)(2,1)S(1)}, u32[]{:S(2)}, u32[]{:S(2)}) collective-permute-start(bf16[304,1792]{1,0:T(8,128)(2,1)S(1)} %slice.100), channel_id=1, source_target_pairs={{0,96},{16,48},{32,0},{48,80},{64,32},{80,112},{96,64},{112,16},{1... | collective-permute-start | bytes 3268616 | tf_op jit(solution)/shard_map/ppermute | solution.py:144
  261.6 14.2 %collective-permute-start.29 = (bf16[128,1792]{1,0:T(8,128)(2,1)S(1)}, bf16[128,1792]{1,0:T(8,128)(2,1)S(1)}, u32[]{:S(2)}, u32[]{:S(2)}) collective-permute-start(bf16[128,1792]{1,0:T(8,128)(2,1)S(1)} %get-tuple-element.39), channel_id=1, source_target_pairs={{0,2},{1,3},{2,4},{3,5},{4,6},{5,7},{6,0},{7,1},{8,10},{9,11},{10,... | collective-permute-start | bytes 1376264 | tf_op jit(solution)/shard_map/ppermute | solution.py:26
  263.6 22.6 %collective-permute-start.28 = (bf16[128,1792]{1,0:T(8,128)(2,1)S(1)}, bf16[128,1792]{1,0:T(8,128)(2,1)S(1)}, u32[]{:S(2)}, u32[]{:S(2)}) collective-permute-start(bf16[128,1792]{1,0:T(8,128)(2,1)S(1)} %get-tuple-element.39), channel_id=1, source_target_pairs={{0,4},{1,5},{2,6},{3,7},{4,0},{5,1},{6,2},{7,3},{8,12},{9,13},{10,... | collective-permute-start | bytes 1376264 | tf_op jit(solution)/shard_map/ppermute | solution.py:26
  266.8 19.4 %collective-permute-start.27 = (bf16[128,1792]{1,0:T(8,128)(2,1)S(1)}, bf16[128,1792]{1,0:T(8,128)(2,1)S(1)}, u32[]{:S(2)}, u32[]{:S(2)}) collective-permute-start(bf16[128,1792]{1,0:T(8,128)(2,1)S(1)} %get-tuple-element.39), channel_id=1, source_target_pairs={{0,6},{1,7},{2,0},{3,1},{4,2},{5,3},{6,4},{7,5},{8,14},{9,15},{10,... | collective-permute-start | bytes 1376264 | tf_op jit(solution)/shard_map/ppermute | solution.py:26
  266.9 29.2 %collective-permute-start.20 = (bf16[288,1792]{1,0:T(8,128)(2,1)S(1)}, bf16[288,1792]{1,0:T(8,128)(2,1)S(1)}, u32[]{:S(2)}, u32[]{:S(2)}) collective-permute-start(bf16[288,1792]{1,0:T(8,128)(2,1)S(1)} %slice.101), channel_id=1, source_target_pairs={{0,96},{16,48},{32,0},{48,80},{64,32},{80,112},{96,64},{112,16},{1... | collective-permute-start | bytes 3096584 | tf_op jit(solution)/shard_map/ppermute | solution.py:144
  286.3 11.8 %collective-permute-start.30 = (bf16[512,1792]{1,0:T(8,128)(2,1)S(1)}, bf16[512,1792]{1,0:T(8,128)(2,1)S(1)}, u32[]{:S(2)}, u32[]{:S(2)}) collective-permute-start(bf16[512,1792]{1,0:T(8,128)(2,1)S(1)} %pad_maximum_fusion.2), channel_id=1, source_target_pairs={{0,1},{1,0},{2,3},{3,2},{4,5},{5,4},{6,7},{7,6},{8,9},{9,8},{10,11... | collective-permute-start | bytes 5505032 | tf_op jit(solution)/shard_map/ppermute | solution.py:26
  287.1 48.6 %collective-permute-start.19 = (bf16[304,1792]{1,0:T(8,128)(2,1)S(1)}, bf16[304,1792]{1,0:T(8,128)(2,1)S(1)}, u32[]{:S(2)}, u32[]{:S(2)}) collective-permute-start(bf16[304,1792]{1,0:T(8,128)(2,1)S(1)} %add_convert_fusion.2), channel_id=1, source_target_pairs={{0,16},{16,0},{32,48},{48,32},{64,80},{80,64},{96,112},{112,96},{1... | collective-permute-start | bytes 3268616 | tf_op jit(solution)/shard_map/ppermute | solution.py:149
  296.5 39.2 %collective-permute-start.21 = (bf16[288,1792]{1,0:T(8,128)(2,1)S(1)}, bf16[288,1792]{1,0:T(8,128)(2,1)S(1)}, u32[]{:S(2)}, u32[]{:S(2)}) collective-permute-start(bf16[288,1792]{1,0:T(8,128)(2,1)S(1)} %add_convert_fusion.4), channel_id=1, source_target_pairs={{0,16},{16,0},{32,48},{48,32},{64,80},{80,64},{96,112},{112,96},{1... | collective-permute-start | bytes 3096584 | tf_op jit(solution)/shard_map/ppermute | solution.py:149
  335.7 6.1 %copy-start.1 = (s32[8,1024]{1,0:T(8,128)S(1)}, s32[8,1024]{1,0:T(8,128)}, u32[]{:S(2)}) copy-start(s32[8,1024]{1,0:T(8,128)} %param.15) | copy-start | bytes 98308
where the time goes:
time: 343 us; the launch traced here: 342 us
  waiting for transfers between devices  212 us (62%)
  starting transfers between devices  43 us (13%)
  local copies, waits for them, and re-layouts  27.7 us (8%)
  matrix products  25.7 us (7%)
  other arithmetic  16.3 us (5%)
  Pallas kernels  11.3 us (3%)
  between operations  6.03 us (2%)
    ppermute x23, waiting for transfers between devices, send(): return lax.ppermute(array, 'tp', tp_shift(dx, dy, dc))  116 us
    ppermute x4, waiting for transfers between devices, along_x(): return lax.ppermute(both, 'blk', xmove)  76 us
    ppermute x23, starting transfers between devices, send(): return lax.ppermute(array, 'tp', tp_shift(dx, dy, dc))  30 us
    ppermute x4, waiting for transfers between devices, along_z(): out.append(lax.ppermute(half[s], 'blk', zmove))  19.7 us
    dot_general x2, matrix products, gradient(): return scale * jnp.dot(hidden_t, resid, preferred_element_type=F32)  12.5 us
    pallas_call x1, Pallas kernels, make_hidden(): pl.pallas_call(hidden_kernel, out_shape=(jax.ShapeDtypeStruct((tokens, un...  11.3 us
    unnamed x35, local copies, waits for them, and re-layouts  11.3 us
    dot_general x2, matrix products, partial_out(): out = scale * jnp.dot(hidden, half, preferred_element_type=F32)  10.1 us
  transfers between devices with their start and end apart: 31, of which 22 were waited for; matrix products, arithmetic and copies ran while one was open for 10% of the time, Pallas kernels for 3%

commit v1 on v0

--- a/solution.py
+++ b/solution.py
@@ -83,6 +83,32 @@
     )(feature_order, token_order, plane, other, gate_t, up_t)
 
 
+def stack_kernel(*refs):
+    count = len(refs) - 2
+    out, sems = refs[count], refs[count + 1]
+    rows = refs[0].shape[0]
+    copies = [
+        pltpu.make_async_copy(refs[i], out.at[pl.ds(i * rows, rows)], sems.at[i])
+        for i in range(count)
+    ]
+    for copy in copies:
+        copy.start()
+    for copy in copies:
+        copy.wait()
+
+
+def stack(parts):
+    rows, width = parts[0].shape
+    return pl.pallas_call(
+        stack_kernel,
+        out_shape=jax.ShapeDtypeStruct((rows * len(parts), width), parts[0].dtype),
+        in_specs=[pl.BlockSpec(memory_space=pl.ANY)] * len(parts),
+        out_specs=pl.BlockSpec(memory_space=pl.ANY),
+        scratch_shapes=[pltpu.SemaphoreType.DMA((len(parts),))],
+        name="stack",
+    )(*parts)
+
+
 def total(*terms):
     out = terms[0].astype(F32)
     for term in terms[1:]:
@@ -121,8 +147,8 @@
     weight_next, weight_prev = edge(0), edge(agents - 1)
     weight_self = 1.0 - weight_next - weight_prev
     odd = place % 2 == 1
-    coef_own = jnp.where(odd, weight_prev, weight_next)
-    coef_got = jnp.where(odd, edge(agents - 2), edge(1))
+    weight_near = jnp.where(odd, weight_prev, weight_next)
+    weight_far = jnp.where(odd, weight_next, weight_prev)
     agent = jnp.sum(jnp.where(slots == place, cycle_order, 0))
     batch = lax.dynamic_slice_in_dim(batch_ids, agent, 1, 0)[0]
 
@@ -133,29 +159,27 @@
     token_order = (core + order // NY) % NC * NY + (y + order % NY) % NY
 
     hidden_dev, features = gate_weight.shape[1], gate_weight.shape[0]
-    cut = (hidden_dev // 2 + 15) // 16 * 16
-    pieces = [slice(0, cut), slice(cut, hidden_dev)]
-    zmove = [(i, (i + 2) % agents if i % 2 else (i - 2) % agents) for i in range(agents)]
+    ends = [0] + [(hidden_dev * n // 3 + 15) // 16 * 16 for n in (1, 2)] + [hidden_dev]
+    pieces = [slice(*e) for e in zip(ends, ends[1:])]
+    zmove = [(i, (i - 2) % agents if i % 2 else (i + 2) % agents) for i in range(agents)]
     xmove = [(i, i ^ 1) for i in range(agents)]
 
-    def along_z(half):
-        out = []
-        for s in pieces:
-            out.append(lax.ppermute(half[s], "blk", zmove))
-        return out
-
-    def along_x(half, got, i):
-        both = total(coef_own * half[pieces[i]].astype(F32), coef_got * got.astype(F32)).astype(BF)
-        return lax.ppermute(both, "blk", xmove)
+    def neighbours(half):
+        near, far = [], []
+        for i, s in enumerate(pieces):
+            near.append(lax.ppermute(half[s], "blk", xmove))
+            far.append(lax.ppermute(near[i], "blk", zmove))
+        near, far = jnp.concatenate(near, axis=0), jnp.concatenate(far, axis=0)
+        return weight_near * near.astype(F32) + weight_far * far.astype(F32)
 
     rows = jnp.take(input_pool, batch, axis=0).T
-    rows, field = barrier((rows, params[0]))
+    rows, field, batch = barrier((rows, params[0], batch))
     field_half = field.astype(BF)
-    partner = send(rows, 1, 0, 0)
-    got = along_z(field_half)
-    partner, batch = barrier((partner, batch))
-    pair = jnp.concatenate([rows, partner], axis=0)
-    parts = [send(pair, 0, -d, 0) for d in (1, 3, 2)]
+    parts = [
+        rows if dx + dy == 0 else send(rows, -dx, -dy, 0)
+        for dy in range(NY)
+        for dx in range(NX)
+    ]
 
     batch_rel = jnp.take(batch.reshape(NC * NY, -1), token_order, axis=0).reshape(-1)
     teacher = jnp.take(teacher_pool, batch_rel, axis=0)
@@ -167,15 +191,11 @@
     teacher_wide = jnp.dot(teacher, place_in, preferred_element_type=F32).astype(BF)
 
     parts, teacher_wide = barrier((parts, teacher_wide))
-    plane = jnp.concatenate([pair, parts[0], parts[2], parts[1]], axis=0)
-    plane, got[0] = barrier((plane, got[0]))
+    plane = stack(parts)
     other = send(plane, 0, 0, 1)
-    side = [along_x(field_half, got[0], 0)]
     hidden, hidden_t = make_hidden(
         feature_order, token_order, plane, other, gate_weight.T, up_weight.T
     )
-    hidden, got[1] = barrier((hidden, got[1]))
-    side.append(along_x(field_half, got[1], 1))
     scale = float(hidden_dev * groups) ** (-0.5)
 
     def partial_out(half):
@@ -186,16 +206,14 @@
         return scale * jnp.dot(hidden_t, resid, preferred_element_type=F32)
 
     resid = sum_over_units(partial_out(field_half))
-    mixed = weight_self * field + jnp.concatenate(side, axis=0).astype(F32)
+    mixed = weight_self * field + neighbours(field_half)
     first = gradient(resid)
     combined = mixed - (2.0 * step) * first
-    combined_half = combined.astype(BF)
-    got = along_z(combined_half)
+    around = neighbours(combined.astype(BF))
     moved = (mixed - step * first).astype(BF)
     base = weight_self * combined + step * first
-    side = [along_x(combined_half, g, i) for i, g in enumerate(got)]
     second = gradient(sum_over_units(partial_out(moved)))
-    return (base + jnp.concatenate(side, axis=0).astype(F32) - step * second)[None]
+    return (base + around - step * second)[None]
 
 
 def solution(mesh):

time: 343 us -> 408 us (1.19)
  Pallas kernels: 11.3 us -> 68.2 us
  waiting for transfers between devices: 212 us -> 230 us
  local copies, waits for them, and re-layouts: 27.7 us -> 18.4 us
  starting transfers between devices: 43 us -> 50.5 us
  other arithmetic: 16.3 us -> 10.1 us
    pallas_call x0 -> x1, Pallas kernels: none -> 56.8 us  [stack(): pl.pallas_call(stack_kernel, out_shape=jax.ShapeDtypeStruct((rows * len(p...]
    ppermute x8 -> x12, waiting for transfers between devices: 95.7 us -> 114 us  [the longest x6 58.5 us: neighbours(): far.append(lax.ppermute(near[i], 'blk', zmove))]
    ppermute x23 -> x26, starting transfers between devices: 30 us -> 36.6 us  [send(): return lax.ppermute(array, 'tp', tp_shift(dx, dy, dc))]
    unnamed x35 -> x36, local copies, waits for them, and re-layouts: 11.3 us -> 5.57 us
    convert_element_type x4 -> x0, other arithmetic: 4.96 us -> none  [along_x(): total(coef_own * half[pieces[i]].astype(F32), coef_got * got.astype(F32))]
    ppermute x8 -> x12, starting transfers between devices: 12.9 us -> 13.9 us  [the longest x6 7.3 us: neighbours(): far.append(lax.ppermute(near[i], 'blk', zmove))]
    ppermute x23 -> x26, waiting for transfers between devices: 116 us -> 116 us  [send(): return lax.ppermute(array, 'tp', tp_shift(dx, dy, dc))]
  transfers between devices with their start and end apart: 31 -> 38, of which waited for: 22 -> 25; matrix products, arithmetic and copies ran while one was open for 10% -> 5% of each run, Pallas kernels for 3% -> 0%
where the time goes in v1:
time: 408 us; the launch traced here: 407 us
  waiting for transfers between devices  230 us (56%)
  Pallas kernels  68.2 us (17%)
  starting transfers between devices  50.5 us (12%)
  matrix products  24.9 us (6%)
  local copies, waits for them, and re-layouts  18.4 us (5%)
  other arithmetic  10.1 us (2%)
  between operations  5.76 us (1%)
    ppermute x26, waiting for transfers between devices, send(): return lax.ppermute(array, 'tp', tp_shift(dx, dy, dc))  116 us
    ppermute x6, waiting for transfers between devices, neighbours(): far.append(lax.ppermute(near[i], 'blk', zmove))  58.5 us
    pallas_call x1, Pallas kernels, stack(): pl.pallas_call(stack_kernel, out_shape=jax.ShapeDtypeStruct((rows * len(p...  56.8 us
    ppermute x6, waiting for transfers between devices, neighbours(): near.append(lax.ppermute(half[s], 'blk', xmove))  55.4 us
    ppermute x26, starting transfers between devices, send(): return lax.ppermute(array, 'tp', tp_shift(dx, dy, dc))  36.6 us
    dot_general x2, matrix products, gradient(): return scale * jnp.dot(hidden_t, resid, preferred_element_type=F32)  13.1 us
    pallas_call x1, Pallas kernels, make_hidden(): pl.pallas_call(hidden_kernel, out_shape=(jax.ShapeDtypeStruct((tokens, un...  11.4 us
    dot_general x2, matrix products, partial_out(): out = scale * jnp.dot(hidden, half, preferred_element_type=F32)  8.78 us
  transfers between devices with their start and end apart: 38, of which 25 were waited for; matrix products, arithmetic and copies ran while one was open for 5% of the time, Pallas kernels for 0%

profile of v1, /device:TPU:0, one launch (start us, length us, event | category | flops | bytes accessed | tf_op | source)
XLA Modules:
  0.0 407.5 jit_solution(379234140659697246)
XLA Ops:
  0.0 1.4 fusion.21
  3.4 1.6 copy.9
  5.0 3.2 gather_fusion.1
  8.4 5.8 %collective-permute-start.10 = (bf16[112,1024]{1,0:T(8,128)(2,1)S(1)}, bf16[112,1024]{1,0:T(8,128)(2,1)S(1)}, u32[]{:S(2)}, u32[]{:S(2)}) collective-permute-start(bf16[112,1024]{1,0:T(8,128)(2,1)S(1)} %select_bitcast_fusion.refs_0_), channel_id=1, source_target_pairs={{0,12},{1,13},{2,14},{3,15},{4,8},{5,9},{6,10},{7,11},{8,4},{9,5},... | collective-permute-start | bytes 688136 | tf_op jit(solution)/shard_map/ppermute | solution.py:26
  15.0 3.0 collective-permute-start.6
  17.9 3.2 collective-permute-start.7
  23.1 3.2 gather_fusion.2
  26.4 1.4 collective-permute-start.8
  27.7 2.0 collective-permute-done.11.refs_6_
  29.8 2.4 collective-permute-start.9
  32.2 3.0 convolution_convert_fusion
  35.7 3.1 collective-permute-done.9.refs_4_
  39.5 56.8 %stack.1.plane_ref = bf16[896,1024]{1,0:T(8,128)(2,1)} custom-call(bf16[112,1024]{1,0:T(8,128)(2,1)} %copy-done.3, bf16[112,1024]{1,0:T(8,128)(2,1)} %copy-done.8, bf16[112,1024]{1,0:T(8,128)(2,1)} %collective-permute-done.7.refs_2_, bf16[112,1024]{1,0:T(8,128)(2,1)} %copy-done.9, bf16[112,1024]{1,0:T(8,128)(2,1)} %copy-done.10, ...), custom_call_target="tpu_custom_call" | custom-call | tf_op jit(solution)/shard_map/stack/pallas_call | solution.py:102
  96.4 2.4 convert_element_type.101
  99.4 1.2 collective-permute-done.13.other_ref
  100.5 11.4 %make_hidden.1 = (bf16[1024,592]{1,0:T(8,128)(2,1)}, bf16[592,1024]{1,0:T(8,128)(2,1)}) custom-call(s32[16]{0:T(128)} %fusion.11.feature_ref, s32[8]{0:T(128)} %get-tuple-element.43.token_ref, bf16[896,1024]{1,0:T(8,128)(2,1)} %stack.1.plane_ref, bf16[896,1024]{1,0:T(8,128)(2,1)} %collective-permute-done.13.other_ref, bf16[592,1792]{1,0:T(8,128)(2,1)} %bitcast.29, ...), custom_call_target="tpu_custom_call" | custom-call | flops 4345298944 | bytes 10338304 | tf_op jit(solution)/shard_map/make_hidden/pallas_call | solution.py:56
  111.9 5.4 %fusion = bf16[1024,1792]{1,0:T(8,128)(2,1)S(1)} fusion(bf16[1024,1792]{1,0:T(8,128)(2,1)} %convolution_convert_fusion, bf16[1024,592]{1,0:T(8,128)(2,1)} %get-tuple-element.32, bf16[592,1792]{1,0:T(8,128)(2,1)S(1)} %convert_element_type.101), kind=kOutput, calls=%fused_computation.5 | convolution fusion | flops 2179989504 | bytes 10674176 | tf_op jit(solution)/shard_map/dot_general | solution.py:202
  117.6 3.6 collective-permute-done.14
  121.8 2.4 collective-permute-start.15
  124.1 2.2 collective-permute-start.16
  126.3 1.4 collective-permute-start.17
  127.7 9.4 %collective-permute-done.15 = bf16[128,1792]{1,0:T(8,128)(2,1)S(1)} collective-permute-done((bf16[128,1792]{1,0:T(8,128)(2,1)S(1)}, bf16[128,1792]{1,0:T(8,128)(2,1)S(1)}, u32[]{:S(2)}, u32[]{:S(2)}) %collective-permute-start.15) | collective-permute-done | bytes 458784 | tf_op jit(solution)/shard_map/ppermute | solution.py:26
  137.0 9.2 %collective-permute-done.16 = bf16[128,1792]{1,0:T(8,128)(2,1)S(1)} collective-permute-done((bf16[128,1792]{1,0:T(8,128)(2,1)S(1)}, bf16[128,1792]{1,0:T(8,128)(2,1)S(1)}, u32[]{:S(2)}, u32[]{:S(2)}) %collective-permute-start.16) | collective-permute-done | bytes 458784 | tf_op jit(solution)/shard_map/ppermute | solution.py:26
  146.2 1.8 collective-permute-done.17
  148.4 2.7 collective-permute-start.18
  151.0 10.6 %collective-permute-done.18 = bf16[128,1792]{1,0:T(8,128)(2,1)S(1)} collective-permute-done((bf16[128,1792]{1,0:T(8,128)(2,1)S(1)}, bf16[128,1792]{1,0:T(8,128)(2,1)S(1)}, u32[]{:S(2)}, u32[]{:S(2)}) %collective-permute-start.18) | collective-permute-done | bytes 458784 | tf_op jit(solution)/shard_map/ppermute | solution.py:26
  161.7 1.2 constant_dynamic-update-slice_fusion.4
  162.8 1.9 collective-permute-start.19
  164.7 1.1 collective-permute-start.20
  165.8 0.9 slice.94
  166.7 1.5 collective-permute-start
  168.2 14.7 %collective-permute-done.19 = bf16[128,1792]{1,0:T(8,128)(2,1)S(1)} collective-permute-done((bf16[128,1792]{1,0:T(8,128)(2,1)S(1)}, bf16[128,1792]{1,0:T(8,128)(2,1)S(1)}, u32[]{:S(2)}, u32[]{:S(2)}) %collective-permute-start.19) | collective-permute-done | bytes 458784 | tf_op jit(solution)/shard_map/ppermute | solution.py:26
  182.9 3.7 collective-permute-done.21
  186.6 1.4 pad_maximum_fusion
  188.0 1.2 fusion.43
  189.2 1.5 collective-permute-start.1
  195.3 12.5 %collective-permute-done.1 = bf16[192,1792]{1,0:T(8,128)(2,1)S(1)} collective-permute-done((bf16[192,1792]{1,0:T(8,128)(2,1)}, bf16[192,1792]{1,0:T(8,128)(2,1)S(1)}, u32[]{:S(2)}, u32[]{:S(2)}) %collective-permute-start.1) | collective-permute-done | bytes 688160 | tf_op jit(solution)/shard_map/ppermute | solution.py:170
  207.8 1.9 collective-permute-start.4
  209.7 12.4 %collective-permute-done.2 = bf16[192,1792]{1,0:T(8,128)(2,1)S(1)} collective-permute-done((bf16[192,1792]{1,0:T(8,128)(2,1)}, bf16[192,1792]{1,0:T(8,128)(2,1)S(1)}, u32[]{:S(2)}, u32[]{:S(2)}) %collective-permute-start.2) | collective-permute-done | bytes 688160 | tf_op jit(solution)/shard_map/ppermute | solution.py:170
  222.0 1.9 collective-permute-start.5
  224.0 1.9 collective-permute-start.3
  228.4 2.8 constant_dynamic-update-slice_fusion
  231.2 11.2 %collective-permute-done.5 = bf16[192,1792]{1,0:T(8,128)(2,1)S(1)} collective-permute-done((bf16[192,1792]{1,0:T(8,128)(2,1)S(1)}, bf16[192,1792]{1,0:T(8,128)(2,1)S(1)}, u32[]{:S(2)}, u32[]{:S(2)}) %collective-permute-start.5) | collective-permute-done | bytes 688160 | tf_op jit(solution)/shard_map/ppermute | solution.py:171
  242.4 14.9 %collective-permute-done.3 = bf16[208,1792]{1,0:T(8,128)(2,1)S(1)} collective-permute-done((bf16[208,1792]{1,0:T(8,128)(2,1)}, bf16[208,1792]{1,0:T(8,128)(2,1)S(1)}, u32[]{:S(2)}, u32[]{:S(2)}) %collective-permute-start.3) | collective-permute-done | bytes 745504 | tf_op jit(solution)/shard_map/ppermute | solution.py:171
  257.3 7.9 %fusion.3 = (bf16[592,1792]{1,0:T(8,128)(2,1)S(1)}, f32[592,1792]{1,0:T(8,128)S(1)}, f32[592,1792]{1,0:T(8,128)S(1)}) fusion(bf16[192,1792]{1,0:T(8,128)(2,1)S(1)} %collective-permute-done.5, bf16[192,1792]{1,0:T(8,128)(2,1)S(1)} %collective-permute-done.4, bf16[208,1792]{1,0:T(8,128)(2,1)S(1)} %collective-permute-done.3, f32[]{:T(128)S(6)} %select_n.182, ...), kind=kOutput, calls=%fused_computation.15 | convolution fusion | flops 2193866752 | bytes 23977996 | tf_op jit(solution)/shard_map/dot_general | solution.py:206
  265.2 3.4 fusion.1
  268.9 3.8 collective-permute-done.29
  273.2 3.2 collective-permute-start.31
  276.4 20.4 %collective-permute-done.30 = bf16[128,1792]{1,0:T(8,128)(2,1)S(1)} collective-permute-done((bf16[128,1792]{1,0:T(8,128)(2,1)S(1)}, bf16[128,1792]{1,0:T(8,128)(2,1)S(1)}, u32[]{:S(2)}, u32[]{:S(2)}) %collective-permute-start.30) | collective-permute-done | bytes 458784 | tf_op jit(solution)/shard_map/ppermute | solution.py:26
  297.1 1.1 collective-permute-start.33
  298.2 12.2 %collective-permute-done.33 = bf16[128,1792]{1,0:T(8,128)(2,1)S(1)} collective-permute-done((bf16[128,1792]{1,0:T(8,128)(2,1)S(1)}, bf16[128,1792]{1,0:T(8,128)(2,1)S(1)}, u32[]{:S(2)}, u32[]{:S(2)}) %collective-permute-start.33) | collective-permute-done | bytes 458784 | tf_op jit(solution)/shard_map/ppermute | solution.py:26
  310.8 2.7 collective-permute-start.34
  314.5 1.0 collective-permute-start.23
  315.5 16.0 %collective-permute-done.34 = bf16[128,1792]{1,0:T(8,128)(2,1)S(1)} collective-permute-done((bf16[128,1792]{1,0:T(8,128)(2,1)S(1)}, bf16[128,1792]{1,0:T(8,128)(2,1)S(1)}, u32[]{:S(2)}, u32[]{:S(2)}) %collective-permute-start.34) | collective-permute-done | bytes 458784 | tf_op jit(solution)/shard_map/ppermute | solution.py:26
  331.5 3.6 collective-permute-done.36
  335.4 1.0 collective-permute-start.24
  336.4 1.2 collective-permute-start.25
  337.5 16.3 %collective-permute-done.24 = bf16[192,1792]{1,0:T(8,128)(2,1)S(1)} collective-permute-done((bf16[192,1792]{1,0:T(8,128)(2,1)S(1)}, bf16[192,1792]{1,0:T(8,128)(2,1)S(1)}, u32[]{:S(2)}, u32[]{:S(2)}) %collective-permute-start.24) | collective-permute-done | bytes 688160 | tf_op jit(solution)/shard_map/ppermute | solution.py:170
  353.8 14.3 %collective-permute-done.25 = bf16[192,1792]{1,0:T(8,128)(2,1)S(1)} collective-permute-done((bf16[192,1792]{1,0:T(8,128)(2,1)S(1)}, bf16[192,1792]{1,0:T(8,128)(2,1)S(1)}, u32[]{:S(2)}, u32[]{:S(2)}) %collective-permute-start.25) | collective-permute-done | bytes 688160 | tf_op jit(solution)/shard_map/ppermute | solution.py:170
  368.1 1.5 collective-permute-start.26
  369.9 1.7 collective-permute-done.27
  371.6 16.0 %collective-permute-done.28 = bf16[192,1792]{1,0:T(8,128)(2,1)S(1)} collective-permute-done((bf16[192,1792]{1,0:T(8,128)(2,1)S(1)}, bf16[192,1792]{1,0:T(8,128)(2,1)S(1)}, u32[]{:S(2)}, u32[]{:S(2)}) %collective-permute-start.28) | collective-permute-done | bytes 688160 | tf_op jit(solution)/shard_map/ppermute | solution.py:171
  387.6 14.7 %collective-permute-done.26 = bf16[208,1792]{1,0:T(8,128)(2,1)S(1)} collective-permute-done((bf16[208,1792]{1,0:T(8,128)(2,1)S(1)}, bf16[208,1792]{1,0:T(8,128)(2,1)S(1)}, u32[]{:S(2)}, u32[]{:S(2)}) %collective-permute-start.26) | collective-permute-done | bytes 745504 | tf_op jit(solution)/shard_map/ppermute | solution.py:171
  402.3 5.2 %subtract_bitcast_fusion = f32[1,592,1792]{2,1,0:T(8,128)} fusion(f32[592,1792]{1,0:T(8,128)S(1)} %get-tuple-element.54, bf16[192,1792]{1,0:T(8,128)(2,1)S(1)} %collective-permute-done.25, bf16[192,1792]{1,0:T(8,128)(2,1)S(1)} %collective-permute-done.24, bf16[208,1792]{1,0:T(8,128)(2,1)S(1)} %collective-permute-done.23, ...), kind=kOutput, calls=%fused_computation.7 | convolution fusion | flops 2197049344 | bytes 21856268 | tf_op jit(solution)/shard_map/dot_general | solution.py:206
  (90 shorter events, 12.4 us)
Async XLA Ops:
  0.0 3.3 copy-start
  0.0 22.4 %copy-start.4 = (bf16[4096,112]{0,1:T(8,128)(2,1)S(1)}, bf16[4096,112]{0,1:T(8,128)(2,1)}, u32[]{:S(2)}) copy-start(bf16[4096,112]{0,1:T(8,128)(2,1)} %param.11) | copy-start | bytes 2752516
  8.4 26.8 %copy-start.3 = (bf16[112,1024]{1,0:T(8,128)(2,1)}, bf16[112,1024]{1,0:T(8,128)(2,1)S(1)}, u32[]{:S(2)}) copy-start(bf16[112,1024]{1,0:T(8,128)(2,1)S(1)} %select_bitcast_fusion.refs_0_) | copy-start | bytes 688132
  8.4 17.9 %collective-permute-start.10 = (bf16[112,1024]{1,0:T(8,128)(2,1)S(1)}, bf16[112,1024]{1,0:T(8,128)(2,1)S(1)}, u32[]{:S(2)}, u32[]{:S(2)}) collective-permute-start(bf16[112,1024]{1,0:T(8,128)(2,1)S(1)} %select_bitcast_fusion.refs_0_), channel_id=1, source_target_pairs={{0,12},{1,13},{2,14},{3,15},{4,8},{5,9},{6,10},{7,11},{8,4},{9,5},... | collective-permute-start | bytes 688136 | tf_op jit(solution)/shard_map/ppermute | solution.py:26
  14.3 15.5 %collective-permute-start.11 = (bf16[112,1024]{1,0:T(8,128)(2,1)S(1)}, bf16[112,1024]{1,0:T(8,128)(2,1)S(1)}, u32[]{:S(2)}, u32[]{:S(2)}) collective-permute-start(bf16[112,1024]{1,0:T(8,128)(2,1)S(1)} %select_bitcast_fusion.refs_0_), channel_id=1, source_target_pairs={{0,2},{1,3},{2,4},{3,5},{4,6},{5,7},{6,0},{7,1},{8,10},{9,11},{10,... | collective-permute-start | bytes 688136 | tf_op jit(solution)/shard_map/ppermute | solution.py:26
  15.0 20.3 %collective-permute-start.12 = (bf16[112,1024]{1,0:T(8,128)(2,1)S(1)}, bf16[112,1024]{1,0:T(8,128)(2,1)S(1)}, u32[]{:S(2)}, u32[]{:S(2)}) collective-permute-start(bf16[112,1024]{1,0:T(8,128)(2,1)S(1)} %select_bitcast_fusion.refs_0_), channel_id=1, source_target_pairs={{0,10},{1,11},{2,12},{3,13},{4,14},{5,15},{6,8},{7,9},{8,2},{9,3},... | collective-permute-start | bytes 688136 | tf_op jit(solution)/shard_map/ppermute | solution.py:26
  15.0 20.3 %collective-permute-start.6 = (bf16[112,1024]{1,0:T(8,128)(2,1)S(1)}, bf16[112,1024]{1,0:T(8,128)(2,1)S(1)}, u32[]{:S(2)}, u32[]{:S(2)}) collective-permute-start(bf16[112,1024]{1,0:T(8,128)(2,1)S(1)} %select_bitcast_fusion.refs_0_), channel_id=1, source_target_pairs={{0,8},{1,9},{2,10},{3,11},{4,12},{5,13},{6,14},{7,15},{8,0},{9,1},... | collective-permute-start | bytes 688136 | tf_op jit(solution)/shard_map/ppermute | solution.py:26
  17.9 17.3 %collective-permute-start.7 = (bf16[112,1024]{1,0:T(8,128)(2,1)S(1)}, bf16[112,1024]{1,0:T(8,128)(2,1)}, u32[]{:S(2)}, u32[]{:S(2)}) collective-permute-start(bf16[112,1024]{1,0:T(8,128)(2,1)S(1)} %select_bitcast_fusion.refs_0_), channel_id=1, source_target_pairs={{0,6},{1,7},{2,0},{3,1},{4,2},{5,3},{6,4},{7,5},{8,14},{9,15},{10,... | collective-permute-start | bytes 688136 | tf_op jit(solution)/shard_map/ppermute | solution.py:26
  26.4 12.4 %copy-start.5 = (bf16[112,1024]{1,0:T(8,128)(2,1)}, bf16[112,1024]{1,0:T(8,128)(2,1)S(1)}, u32[]{:S(2)}) copy-start(bf16[112,1024]{1,0:T(8,128)(2,1)S(1)} %collective-permute-done.10.refs_5_) | copy-start | bytes 688132
  26.4 9.3 %collective-permute-start.8 = (bf16[112,1024]{1,0:T(8,128)(2,1)S(1)}, bf16[112,1024]{1,0:T(8,128)(2,1)S(1)}, u32[]{:S(2)}, u32[]{:S(2)}) collective-permute-start(bf16[112,1024]{1,0:T(8,128)(2,1)S(1)} %select_bitcast_fusion.refs_0_), channel_id=1, source_target_pairs={{0,14},{1,15},{2,8},{3,9},{4,10},{5,11},{6,12},{7,13},{8,6},{9,7},... | collective-permute-start | bytes 688136 | tf_op jit(solution)/shard_map/ppermute | solution.py:26
  29.8 9.0 %copy-start.6 = (bf16[112,1024]{1,0:T(8,128)(2,1)}, bf16[112,1024]{1,0:T(8,128)(2,1)S(1)}, u32[]{:S(2)}) copy-start(bf16[112,1024]{1,0:T(8,128)(2,1)S(1)} %collective-permute-done.11.refs_6_) | copy-start | bytes 688132
  29.8 9.0 %collective-permute-start.9 = (bf16[112,1024]{1,0:T(8,128)(2,1)S(1)}, bf16[112,1024]{1,0:T(8,128)(2,1)S(1)}, u32[]{:S(2)}, u32[]{:S(2)}) collective-permute-start(bf16[112,1024]{1,0:T(8,128)(2,1)S(1)} %select_bitcast_fusion.refs_0_), channel_id=1, source_target_pairs={{0,4},{1,5},{2,6},{3,7},{4,0},{5,1},{6,2},{7,3},{8,12},{9,13},{10,... | collective-permute-start | bytes 688136 | tf_op jit(solution)/shard_map/ppermute | solution.py:26
  35.2 3.6 copy-start.7
  35.2 3.6 copy-start.8
  35.7 3.1 copy-start.9
  38.8 0.7 copy-start.10
  96.3 4.2 %collective-permute-start.13 = (bf16[896,1024]{1,0:T(8,128)(2,1)}, bf16[896,1024]{1,0:T(8,128)(2,1)}, u32[]{:S(2)}, u32[]{:S(2)}) collective-permute-start(bf16[896,1024]{1,0:T(8,128)(2,1)} %stack.1.plane_ref), channel_id=1, source_target_pairs={{0,1},{1,0},{2,3},{3,2},{4,5},{5,4},{6,7},{7,6},{8,9},{9,8},{10,11... | collective-permute-start | bytes 5505032 | tf_op jit(solution)/shard_map/ppermute | solution.py:26
  117.4 3.9 collective-permute-start.14
  121.8 15.3 %collective-permute-start.15 = (bf16[128,1792]{1,0:T(8,128)(2,1)S(1)}, bf16[128,1792]{1,0:T(8,128)(2,1)S(1)}, u32[]{:S(2)}, u32[]{:S(2)}) collective-permute-start(bf16[128,1792]{1,0:T(8,128)(2,1)S(1)} %get-tuple-element.51), channel_id=1, source_target_pairs={{0,2},{1,3},{2,4},{3,5},{4,6},{5,7},{6,0},{7,1},{8,10},{9,11},{10,... | collective-permute-start | bytes 1376264 | tf_op jit(solution)/shard_map/ppermute | solution.py:26
  124.1 22.1 %collective-permute-start.16 = (bf16[128,1792]{1,0:T(8,128)(2,1)S(1)}, bf16[128,1792]{1,0:T(8,128)(2,1)S(1)}, u32[]{:S(2)}, u32[]{:S(2)}) collective-permute-start(bf16[128,1792]{1,0:T(8,128)(2,1)S(1)} %get-tuple-element.53), channel_id=1, source_target_pairs={{0,6},{1,7},{2,0},{3,1},{4,2},{5,3},{6,4},{7,5},{8,14},{9,15},{10,... | collective-permute-start | bytes 1376264 | tf_op jit(solution)/shard_map/ppermute | solution.py:26
  126.3 21.7 %collective-permute-start.17 = (bf16[128,1792]{1,0:T(8,128)(2,1)S(1)}, bf16[128,1792]{1,0:T(8,128)(2,1)S(1)}, u32[]{:S(2)}, u32[]{:S(2)}) collective-permute-start(bf16[128,1792]{1,0:T(8,128)(2,1)S(1)} %get-tuple-element.52), channel_id=1, source_target_pairs={{0,4},{1,5},{2,6},{3,7},{4,0},{5,1},{6,2},{7,3},{8,12},{9,13},{10,... | collective-permute-start | bytes 1376264 | tf_op jit(solution)/shard_map/ppermute | solution.py:26
  148.4 13.3 %collective-permute-start.18 = (bf16[128,1792]{1,0:T(8,128)(2,1)S(1)}, bf16[128,1792]{1,0:T(8,128)(2,1)S(1)}, u32[]{:S(2)}, u32[]{:S(2)}) collective-permute-start(bf16[128,1792]{1,0:T(8,128)(2,1)S(1)} %fusion.39), channel_id=1, source_target_pairs={{0,8},{1,9},{2,10},{3,11},{4,12},{5,13},{6,14},{7,15},{8,0},{9,1},... | collective-permute-start | bytes 1376264 | tf_op jit(solution)/shard_map/ppermute | solution.py:26
  162.8 28.4 %copy-start.11 = (f32[8]{0:T(128)S(1)}, f32[8]{0:T(128)}, u32[]{:S(2)}) copy-start(f32[8]{0:T(128)} %param.17) | copy-start | bytes 100
  162.8 20.1 %collective-permute-start.19 = (bf16[128,1792]{1,0:T(8,128)(2,1)S(1)}, bf16[128,1792]{1,0:T(8,128)(2,1)S(1)}, u32[]{:S(2)}, u32[]{:S(2)}) collective-permute-start(bf16[128,1792]{1,0:T(8,128)(2,1)S(1)} %get-tuple-element.41), channel_id=1, source_target_pairs={{0,6},{1,7},{2,0},{3,1},{4,2},{5,3},{6,4},{7,5},{8,14},{9,15},{10,... | collective-permute-start | bytes 1376264 | tf_op jit(solution)/shard_map/ppermute | solution.py:26
  164.7 18.2 %collective-permute-start.20 = (bf16[128,1792]{1,0:T(8,128)(2,1)S(1)}, bf16[128,1792]{1,0:T(8,128)(2,1)S(1)}, u32[]{:S(2)}, u32[]{:S(2)}) collective-permute-start(bf16[128,1792]{1,0:T(8,128)(2,1)S(1)} %get-tuple-element.41), channel_id=1, source_target_pairs={{0,4},{1,5},{2,6},{3,7},{4,0},{5,1},{6,2},{7,3},{8,12},{9,13},{10,... | collective-permute-start | bytes 1376264 | tf_op jit(solution)/shard_map/ppermute | solution.py:26
  165.8 20.8 %collective-permute-start.21 = (bf16[128,1792]{1,0:T(8,128)(2,1)S(1)}, bf16[128,1792]{1,0:T(8,128)(2,1)S(1)}, u32[]{:S(2)}, u32[]{:S(2)}) collective-permute-start(bf16[128,1792]{1,0:T(8,128)(2,1)S(1)} %get-tuple-element.41), channel_id=1, source_target_pairs={{0,2},{1,3},{2,4},{3,5},{4,6},{5,7},{6,0},{7,1},{8,10},{9,11},{10,... | collective-permute-start | bytes 1376264 | tf_op jit(solution)/shard_map/ppermute | solution.py:26
  166.7 57.3 %collective-permute-start = (bf16[208,1792]{1,0:T(8,128)(2,1)}, bf16[208,1792]{1,0:T(8,128)(2,1)}, u32[]{:S(2)}, u32[]{:S(2)}) collective-permute-start(bf16[208,1792]{1,0:T(8,128)(2,1)} %slice.94), channel_id=1, source_target_pairs={{0,16},{16,0},{32,48},{48,32},{64,80},{80,64},{96,112},{112,96},{1... | collective-permute-start | bytes 2236424 | tf_op jit(solution)/shard_map/ppermute | solution.py:170
  188.0 40.4 %collective-permute-start.22 = (bf16[512,1792]{1,0:T(8,128)(2,1)}, bf16[512,1792]{1,0:T(8,128)(2,1)}, u32[]{:S(2)}, u32[]{:S(2)}) collective-permute-start(bf16[512,1792]{1,0:T(8,128)(2,1)} %pad_maximum_fusion), channel_id=1, source_target_pairs={{0,1},{1,0},{2,3},{3,2},{4,5},{5,4},{6,7},{7,6},{8,9},{9,8},{10,11... | collective-permute-start | bytes 5505032 | tf_op jit(solution)/shard_map/ppermute | solution.py:26
  189.2 18.5 %collective-permute-start.1 = (bf16[192,1792]{1,0:T(8,128)(2,1)}, bf16[192,1792]{1,0:T(8,128)(2,1)S(1)}, u32[]{:S(2)}, u32[]{:S(2)}) collective-permute-start(bf16[192,1792]{1,0:T(8,128)(2,1)} %get-tuple-element.46), channel_id=1, source_target_pairs={{0,16},{16,0},{32,48},{48,32},{64,80},{80,64},{96,112},{112,96},{1... | collective-permute-start | bytes 2064392 | tf_op jit(solution)/shard_map/ppermute | solution.py:170
  190.8 31.3 %collective-permute-start.2 = (bf16[192,1792]{1,0:T(8,128)(2,1)}, bf16[192,1792]{1,0:T(8,128)(2,1)S(1)}, u32[]{:S(2)}, u32[]{:S(2)}) collective-permute-start(bf16[192,1792]{1,0:T(8,128)(2,1)} %get-tuple-element.47), channel_id=1, source_target_pairs={{0,16},{16,0},{32,48},{48,32},{64,80},{80,64},{96,112},{112,96},{1... | collective-permute-start | bytes 2064392 | tf_op jit(solution)/shard_map/ppermute | solution.py:170
  195.3 62.0 %copy-start.12 = (bf16[592,1024]{1,0:T(8,128)(2,1)S(1)}, bf16[592,1024]{1,0:T(8,128)(2,1)}, u32[]{:S(2)}) copy-start(bf16[592,1024]{1,0:T(8,128)(2,1)} %get-tuple-element.31) | copy-start | bytes 3637252
  207.8 23.4 %collective-permute-start.4 = (bf16[192,1792]{1,0:T(8,128)(2,1)S(1)}, bf16[192,1792]{1,0:T(8,128)(2,1)S(1)}, u32[]{:S(2)}, u32[]{:S(2)}) collective-permute-start(bf16[192,1792]{1,0:T(8,128)(2,1)S(1)} %collective-permute-done.1), channel_id=1, source_target_pairs={{0,32},{16,112},{32,64},{48,16},{64,96},{80,48},{96,0},{112,80},{1... | collective-permute-start | bytes 2064392 | tf_op jit(solution)/shard_map/ppermute | solution.py:171
  222.0 20.3 %collective-permute-start.5 = (bf16[192,1792]{1,0:T(8,128)(2,1)S(1)}, bf16[192,1792]{1,0:T(8,128)(2,1)S(1)}, u32[]{:S(2)}, u32[]{:S(2)}) collective-permute-start(bf16[192,1792]{1,0:T(8,128)(2,1)S(1)} %collective-permute-done.2), channel_id=1, source_target_pairs={{0,32},{16,112},{32,64},{48,16},{64,96},{80,48},{96,0},{112,80},{1... | collective-permute-start | bytes 2064392 | tf_op jit(solution)/shard_map/ppermute | solution.py:171
  224.0 33.3 %collective-permute-start.3 = (bf16[208,1792]{1,0:T(8,128)(2,1)}, bf16[208,1792]{1,0:T(8,128)(2,1)S(1)}, u32[]{:S(2)}, u32[]{:S(2)}) collective-permute-start(bf16[208,1792]{1,0:T(8,128)(2,1)} %collective-permute-done), channel_id=1, source_target_pairs={{0,32},{16,112},{32,64},{48,16},{64,96},{80,48},{96,0},{112,80},{1... | collective-permute-start | bytes 2236424 | tf_op jit(solution)/shard_map/ppermute | solution.py:171
  257.3 7.9 %copy-start.2 = (bf16[1024,1792]{1,0:T(8,128)(2,1)S(1)}, bf16[1024,1792]{1,0:T(8,128)(2,1)}, u32[]{:S(2)}) copy-start(bf16[1024,1792]{1,0:T(8,128)(2,1)} %convolution_convert_fusion) | copy-start | bytes 11010052
  257.3 7.9 %copy-start.13 = (bf16[1024,592]{1,0:T(8,128)(2,1)S(1)}, bf16[1024,592]{1,0:T(8,128)(2,1)}, u32[]{:S(2)}) copy-start(bf16[1024,592]{1,0:T(8,128)(2,1)} %get-tuple-element.32) | copy-start | bytes 3637252
  268.8 3.9 collective-permute-start.29
  273.1 23.7 %collective-permute-start.30 = (bf16[128,1792]{1,0:T(8,128)(2,1)S(1)}, bf16[128,1792]{1,0:T(8,128)(2,1)S(1)}, u32[]{:S(2)}, u32[]{:S(2)}) collective-permute-start(bf16[128,1792]{1,0:T(8,128)(2,1)S(1)} %get-tuple-element.48), channel_id=1, source_target_pairs={{0,2},{1,3},{2,4},{3,5},{4,6},{5,7},{6,0},{7,1},{8,10},{9,11},{10,... | collective-permute-start | bytes 1376264 | tf_op jit(solution)/shard_map/ppermute | solution.py:26
  273.2 23.6 %collective-permute-start.31 = (bf16[128,1792]{1,0:T(8,128)(2,1)S(1)}, bf16[128,1792]{1,0:T(8,128)(2,1)S(1)}, u32[]{:S(2)}, u32[]{:S(2)}) collective-permute-start(bf16[128,1792]{1,0:T(8,128)(2,1)S(1)} %get-tuple-element.50), channel_id=1, source_target_pairs={{0,6},{1,7},{2,0},{3,1},{4,2},{5,3},{6,4},{7,5},{8,14},{9,15},{10,... | collective-permute-start | bytes 1376264 | tf_op jit(solution)/shard_map/ppermute | solution.py:26
  276.4 20.4 %collective-permute-start.32 = (bf16[128,1792]{1,0:T(8,128)(2,1)S(1)}, bf16[128,1792]{1,0:T(8,128)(2,1)S(1)}, u32[]{:S(2)}, u32[]{:S(2)}) collective-permute-start(bf16[128,1792]{1,0:T(8,128)(2,1)S(1)} %get-tuple-element.49), channel_id=1, source_target_pairs={{0,4},{1,5},{2,6},{3,7},{4,0},{5,1},{6,2},{7,3},{8,12},{9,13},{10,... | collective-permute-start | bytes 1376264 | tf_op jit(solution)/shard_map/ppermute | solution.py:26
  297.1 13.3 %collective-permute-start.33 = (bf16[128,1792]{1,0:T(8,128)(2,1)S(1)}, bf16[128,1792]{1,0:T(8,128)(2,1)S(1)}, u32[]{:S(2)}, u32[]{:S(2)}) collective-permute-start(bf16[128,1792]{1,0:T(8,128)(2,1)S(1)} %fusion.40), channel_id=1, source_target_pairs={{0,8},{1,9},{2,10},{3,11},{4,12},{5,13},{6,14},{7,15},{8,0},{9,1},... | collective-permute-start | bytes 1376264 | tf_op jit(solution)/shard_map/ppermute | solution.py:26
  310.8 20.7 %collective-permute-start.34 = (bf16[128,1792]{1,0:T(8,128)(2,1)S(1)}, bf16[128,1792]{1,0:T(8,128)(2,1)S(1)}, u32[]{:S(2)}, u32[]{:S(2)}) collective-permute-start(bf16[128,1792]{1,0:T(8,128)(2,1)S(1)} %get-tuple-element.39), channel_id=1, source_target_pairs={{0,6},{1,7},{2,0},{3,1},{4,2},{5,3},{6,4},{7,5},{8,14},{9,15},{10,... | collective-permute-start | bytes 1376264 | tf_op jit(solution)/shard_map/ppermute | solution.py:26
  313.5 18.0 %collective-permute-start.35 = (bf16[128,1792]{1,0:T(8,128)(2,1)S(1)}, bf16[128,1792]{1,0:T(8,128)(2,1)S(1)}, u32[]{:S(2)}, u32[]{:S(2)}) collective-permute-start(bf16[128,1792]{1,0:T(8,128)(2,1)S(1)} %get-tuple-element.39), channel_id=1, source_target_pairs={{0,4},{1,5},{2,6},{3,7},{4,0},{5,1},{6,2},{7,3},{8,12},{9,13},{10,... | collective-permute-start | bytes 1376264 | tf_op jit(solution)/shard_map/ppermute | solution.py:26
  313.8 21.3 %collective-permute-start.36 = (bf16[128,1792]{1,0:T(8,128)(2,1)S(1)}, bf16[128,1792]{1,0:T(8,128)(2,1)S(1)}, u32[]{:S(2)}, u32[]{:S(2)}) collective-permute-start(bf16[128,1792]{1,0:T(8,128)(2,1)S(1)} %get-tuple-element.39), channel_id=1, source_target_pairs={{0,2},{1,3},{2,4},{3,5},{4,6},{5,7},{6,0},{7,1},{8,10},{9,11},{10,... | collective-permute-start | bytes 1376264 | tf_op jit(solution)/shard_map/ppermute | solution.py:26
  314.5 53.6 %collective-permute-start.23 = (bf16[208,1792]{1,0:T(8,128)(2,1)S(1)}, bf16[208,1792]{1,0:T(8,128)(2,1)S(1)}, u32[]{:S(2)}, u32[]{:S(2)}) collective-permute-start(bf16[208,1792]{1,0:T(8,128)(2,1)S(1)} %slice.105), channel_id=1, source_target_pairs={{0,16},{16,0},{32,48},{48,32},{64,80},{80,64},{96,112},{112,96},{1... | collective-permute-start | bytes 2236424 | tf_op jit(solution)/shard_map/ppermute | solution.py:170
  335.2 34.5 %collective-permute-start.37 = (bf16[512,1792]{1,0:T(8,128)(2,1)S(1)}, bf16[512,1792]{1,0:T(8,128)(2,1)S(1)}, u32[]{:S(2)}, u32[]{:S(2)}) collective-permute-start(bf16[512,1792]{1,0:T(8,128)(2,1)S(1)} %pad_maximum_fusion.1), channel_id=1, source_target_pairs={{0,1},{1,0},{2,3},{3,2},{4,5},{5,4},{6,7},{7,6},{8,9},{9,8},{10,11... | collective-permute-start | bytes 5505032 | tf_op jit(solution)/shard_map/ppermute | solution.py:26
  335.4 18.4 %collective-permute-start.24 = (bf16[192,1792]{1,0:T(8,128)(2,1)S(1)}, bf16[192,1792]{1,0:T(8,128)(2,1)S(1)}, u32[]{:S(2)}, u32[]{:S(2)}) collective-permute-start(bf16[192,1792]{1,0:T(8,128)(2,1)S(1)} %get-tuple-element.44), channel_id=1, source_target_pairs={{0,16},{16,0},{32,48},{48,32},{64,80},{80,64},{96,112},{112,96},{1... | collective-permute-start | bytes 2064392 | tf_op jit(solution)/shard_map/ppermute | solution.py:170
  336.4 31.7 %collective-permute-start.25 = (bf16[192,1792]{1,0:T(8,128)(2,1)S(1)}, bf16[192,1792]{1,0:T(8,128)(2,1)S(1)}, u32[]{:S(2)}, u32[]{:S(2)}) collective-permute-start(bf16[192,1792]{1,0:T(8,128)(2,1)S(1)} %get-tuple-element.45), channel_id=1, source_target_pairs={{0,16},{16,0},{32,48},{48,32},{64,80},{80,64},{96,112},{112,96},{1... | collective-permute-start | bytes 2064392 | tf_op jit(solution)/shard_map/ppermute | solution.py:170
  353.8 17.8 %collective-permute-start.27 = (bf16[192,1792]{1,0:T(8,128)(2,1)S(1)}, bf16[192,1792]{1,0:T(8,128)(2,1)S(1)}, u32[]{:S(2)}, u32[]{:S(2)}) collective-permute-start(bf16[192,1792]{1,0:T(8,128)(2,1)S(1)} %collective-permute-done.24), channel_id=1, source_target_pairs={{0,32},{16,112},{32,64},{48,16},{64,96},{80,48},{96,0},{112,80},{1... | collective-permute-start | bytes 2064392 | tf_op jit(solution)/shard_map/ppermute | solution.py:171
  368.1 19.5 %collective-permute-start.28 = (bf16[192,1792]{1,0:T(8,128)(2,1)S(1)}, bf16[192,1792]{1,0:T(8,128)(2,1)S(1)}, u32[]{:S(2)}, u32[]{:S(2)}) collective-permute-start(bf16[192,1792]{1,0:T(8,128)(2,1)S(1)} %collective-permute-done.25), channel_id=1, source_target_pairs={{0,32},{16,112},{32,64},{48,16},{64,96},{80,48},{96,0},{112,80},{1... | collective-permute-start | bytes 2064392 | tf_op jit(solution)/shard_map/ppermute | solution.py:171
  368.1 34.2 %collective-permute-start.26 = (bf16[208,1792]{1,0:T(8,128)(2,1)S(1)}, bf16[208,1792]{1,0:T(8,128)(2,1)S(1)}, u32[]{:S(2)}, u32[]{:S(2)}) collective-permute-start(bf16[208,1792]{1,0:T(8,128)(2,1)S(1)} %collective-permute-done.23), channel_id=1, source_target_pairs={{0,32},{16,112},{32,64},{48,16},{64,96},{80,48},{96,0},{112,80},{1... | collective-permute-start | bytes 2236424 | tf_op jit(solution)/shard_map/ppermute | solution.py:171
  402.3 5.2 %copy-start.1 = (s32[8,1024]{1,0:T(8,128)S(1)}, s32[8,1024]{1,0:T(8,128)}, u32[]{:S(2)}) copy-start(s32[8,1024]{1,0:T(8,128)} %param.15) | copy-start | bytes 98308

commit v2 on v1

--- a/solution.py
+++ b/solution.py
@@ -84,27 +84,23 @@
 
 
 def stack_kernel(*refs):
-    count = len(refs) - 2
-    out, sems = refs[count], refs[count + 1]
+    out = refs[-1]
     rows = refs[0].shape[0]
-    copies = [
-        pltpu.make_async_copy(refs[i], out.at[pl.ds(i * rows, rows)], sems.at[i])
-        for i in range(count)
-    ]
-    for copy in copies:
-        copy.start()
-    for copy in copies:
-        copy.wait()
+    for i, part in enumerate(refs[:-1]):
+        out[i * rows : (i + 1) * rows] = part[...]
 
 
 def stack(parts):
     rows, width = parts[0].shape
+    tile = width // 2
+    size = 2 * rows * len(parts) * width * parts[0].dtype.itemsize
     return pl.pallas_call(
         stack_kernel,
         out_shape=jax.ShapeDtypeStruct((rows * len(parts), width), parts[0].dtype),
-        in_specs=[pl.BlockSpec(memory_space=pl.ANY)] * len(parts),
-        out_specs=pl.BlockSpec(memory_space=pl.ANY),
-        scratch_shapes=[pltpu.SemaphoreType.DMA((len(parts),))],
+        grid=(width // tile,),
+        in_specs=[pl.BlockSpec((rows, tile), lambda i: (0, i))] * len(parts),
+        out_specs=pl.BlockSpec((rows * len(parts), tile), lambda i: (0, i)),
+        cost_estimate=pl.CostEstimate(flops=0, transcendentals=0, bytes_accessed=size),
         name="stack",
     )(*parts)
 

time: 408 us -> 354 us (0.87)
  Pallas kernels: 68.2 us -> 14.1 us
    pallas_call x1, Pallas kernels: 56.8 us -> 2.64 us  [stack(): pl.pallas_call(stack_kernel, out_shape=jax.ShapeDtypeStruct((rows * len(p...]
  transfers between devices with their start and end apart: 38 -> 38, of which waited for: 25 -> 25; matrix products, arithmetic and copies ran while one was open for 5% -> 6% of each run, Pallas kernels for 0% -> 0%
where the time goes in v2:
time: 354 us; the launch traced here: 353 us
  waiting for transfers between devices  230 us (65%)
  starting transfers between devices  50.4 us (14%)
  matrix products  24.9 us (7%)
  local copies, waits for them, and re-layouts  18.4 us (5%)
  Pallas kernels  14.1 us (4%)
  other arithmetic  10.1 us (3%)
  between operations  5.74 us (2%)
    ppermute x26, waiting for transfers between devices, send(): return lax.ppermute(array, 'tp', tp_shift(dx, dy, dc))  116 us
    ppermute x6, waiting for transfers between devices, neighbours(): far.append(lax.ppermute(near[i], 'blk', zmove))  58.5 us
    ppermute x6, waiting for transfers between devices, neighbours(): near.append(lax.ppermute(half[s], 'blk', xmove))  55.4 us
    ppermute x26, starting transfers between devices, send(): return lax.ppermute(array, 'tp', tp_shift(dx, dy, dc))  36.5 us
    dot_general x2, matrix products, gradient(): return scale * jnp.dot(hidden_t, resid, preferred_element_type=F32)  13.1 us
    pallas_call x1, Pallas kernels, make_hidden(): pl.pallas_call(hidden_kernel, out_shape=(jax.ShapeDtypeStruct((tokens, un...  11.4 us
    dot_general x2, matrix products, partial_out(): out = scale * jnp.dot(hidden, half, preferred_element_type=F32)  8.78 us
    ppermute x6, starting transfers between devices, neighbours(): far.append(lax.ppermute(near[i], 'blk', zmove))  7.31 us
  transfers between devices with their start and end apart: 38, of which 25 were waited for; matrix products, arithmetic and copies ran while one was open for 6% of the time, Pallas kernels for 0%

profile of v2, /device:TPU:0, one launch (start us, length us, event | category | flops | bytes accessed | tf_op | source)
XLA Modules:
  0.0 353.3 jit_solution(5242116602484564199)
XLA Ops:
  0.0 1.4 fusion.21
  3.4 1.6 copy.9
  5.0 3.2 gather_fusion.1
  8.4 5.8 %collective-permute-start.10 = (bf16[112,1024]{1,0:T(8,128)(2,1)S(1)}, bf16[112,1024]{1,0:T(8,128)(2,1)S(1)}, u32[]{:S(2)}, u32[]{:S(2)}) collective-permute-start(bf16[112,1024]{1,0:T(8,128)(2,1)S(1)} %select_bitcast_fusion.refs_0_), channel_id=1, source_target_pairs={{0,12},{1,13},{2,14},{3,15},{4,8},{5,9},{6,10},{7,11},{8,4},{9,5},... | collective-permute-start | bytes 688136 | tf_op jit(solution)/shard_map/ppermute | solution.py:26
  15.0 3.0 collective-permute-start.6
  17.9 3.2 collective-permute-start.7
  23.1 3.2 gather_fusion.2
  26.4 1.4 collective-permute-start.8
  27.7 2.0 collective-permute-done.11.refs_6_
  29.8 2.4 collective-permute-start.9
  32.2 3.0 convolution_convert_fusion
  35.7 3.1 collective-permute-done.9.refs_4_
  39.5 2.6 stack.1.plane_ref
  42.2 2.4 convert_element_type.101
  45.2 1.2 collective-permute-done.13.other_ref
  46.3 11.4 %make_hidden.1 = (bf16[1024,592]{1,0:T(8,128)(2,1)}, bf16[592,1024]{1,0:T(8,128)(2,1)}) custom-call(s32[16]{0:T(128)} %fusion.11.feature_ref, s32[8]{0:T(128)} %get-tuple-element.43.token_ref, bf16[896,1024]{1,0:T(8,128)(2,1)} %stack.1.plane_ref, bf16[896,1024]{1,0:T(8,128)(2,1)} %collective-permute-done.13.other_ref, bf16[592,1792]{1,0:T(8,128)(2,1)} %bitcast.29, ...), custom_call_target="tpu_custom_call" | custom-call | flops 4345298944 | bytes 10338304 | tf_op jit(solution)/shard_map/make_hidden/pallas_call | solution.py:56
  57.7 5.4 %fusion = bf16[1024,1792]{1,0:T(8,128)(2,1)S(1)} fusion(bf16[1024,1792]{1,0:T(8,128)(2,1)} %convolution_convert_fusion, bf16[1024,592]{1,0:T(8,128)(2,1)} %get-tuple-element.32, bf16[592,1792]{1,0:T(8,128)(2,1)S(1)} %convert_element_type.101), kind=kOutput, calls=%fused_computation.5 | convolution fusion | flops 2179989504 | bytes 10674176 | tf_op jit(solution)/shard_map/dot_general | solution.py:198
  63.4 3.7 %collective-permute-done.14 = bf16[512,1792]{1,0:T(8,128)(2,1)S(1)} collective-permute-done((bf16[512,1792]{1,0:T(8,128)(2,1)S(1)}, bf16[512,1792]{1,0:T(8,128)(2,1)S(1)}, u32[]{:S(2)}, u32[]{:S(2)}) %collective-permute-start.14) | collective-permute-done | bytes 1835040 | tf_op jit(solution)/shard_map/ppermute | solution.py:26
  67.6 2.4 collective-permute-start.15
  69.9 2.2 collective-permute-start.16
  72.1 1.4 collective-permute-start.17
  73.5 9.4 %collective-permute-done.15 = bf16[128,1792]{1,0:T(8,128)(2,1)S(1)} collective-permute-done((bf16[128,1792]{1,0:T(8,128)(2,1)S(1)}, bf16[128,1792]{1,0:T(8,128)(2,1)S(1)}, u32[]{:S(2)}, u32[]{:S(2)}) %collective-permute-start.15) | collective-permute-done | bytes 458784 | tf_op jit(solution)/shard_map/ppermute | solution.py:26
  82.8 9.2 %collective-permute-done.16 = bf16[128,1792]{1,0:T(8,128)(2,1)S(1)} collective-permute-done((bf16[128,1792]{1,0:T(8,128)(2,1)S(1)}, bf16[128,1792]{1,0:T(8,128)(2,1)S(1)}, u32[]{:S(2)}, u32[]{:S(2)}) %collective-permute-start.16) | collective-permute-done | bytes 458784 | tf_op jit(solution)/shard_map/ppermute | solution.py:26
  92.1 1.8 collective-permute-done.17
  94.2 2.7 collective-permute-start.18
  96.8 10.6 %collective-permute-done.18 = bf16[128,1792]{1,0:T(8,128)(2,1)S(1)} collective-permute-done((bf16[128,1792]{1,0:T(8,128)(2,1)S(1)}, bf16[128,1792]{1,0:T(8,128)(2,1)S(1)}, u32[]{:S(2)}, u32[]{:S(2)}) %collective-permute-start.18) | collective-permute-done | bytes 458784 | tf_op jit(solution)/shard_map/ppermute | solution.py:26
  107.5 1.2 constant_dynamic-update-slice_fusion.4
  108.6 1.9 collective-permute-start.19
  110.5 1.1 collective-permute-start.20
  111.6 0.9 slice.94
  112.5 1.5 collective-permute-start
  114.0 14.7 %collective-permute-done.19 = bf16[128,1792]{1,0:T(8,128)(2,1)S(1)} collective-permute-done((bf16[128,1792]{1,0:T(8,128)(2,1)S(1)}, bf16[128,1792]{1,0:T(8,128)(2,1)S(1)}, u32[]{:S(2)}, u32[]{:S(2)}) %collective-permute-start.19) | collective-permute-done | bytes 458784 | tf_op jit(solution)/shard_map/ppermute | solution.py:26
  128.7 3.7 %collective-permute-done.21 = bf16[128,1792]{1,0:T(8,128)(2,1)S(1)} collective-permute-done((bf16[128,1792]{1,0:T(8,128)(2,1)S(1)}, bf16[128,1792]{1,0:T(8,128)(2,1)S(1)}, u32[]{:S(2)}, u32[]{:S(2)}) %collective-permute-start.21) | collective-permute-done | bytes 458784 | tf_op jit(solution)/shard_map/ppermute | solution.py:26
  132.4 1.4 pad_maximum_fusion
  133.8 1.2 fusion.43
  135.0 1.5 collective-permute-start.1
  141.1 12.5 %collective-permute-done.1 = bf16[192,1792]{1,0:T(8,128)(2,1)S(1)} collective-permute-done((bf16[192,1792]{1,0:T(8,128)(2,1)}, bf16[192,1792]{1,0:T(8,128)(2,1)S(1)}, u32[]{:S(2)}, u32[]{:S(2)}) %collective-permute-start.1) | collective-permute-done | bytes 688160 | tf_op jit(solution)/shard_map/ppermute | solution.py:166
  153.6 1.9 collective-permute-start.4
  155.5 12.4 %collective-permute-done.2 = bf16[192,1792]{1,0:T(8,128)(2,1)S(1)} collective-permute-done((bf16[192,1792]{1,0:T(8,128)(2,1)}, bf16[192,1792]{1,0:T(8,128)(2,1)S(1)}, u32[]{:S(2)}, u32[]{:S(2)}) %collective-permute-start.2) | collective-permute-done | bytes 688160 | tf_op jit(solution)/shard_map/ppermute | solution.py:166
  167.8 1.9 collective-permute-start.5
  169.8 1.9 collective-permute-start.3
  174.2 2.8 constant_dynamic-update-slice_fusion
  177.0 11.2 %collective-permute-done.5 = bf16[192,1792]{1,0:T(8,128)(2,1)S(1)} collective-permute-done((bf16[192,1792]{1,0:T(8,128)(2,1)S(1)}, bf16[192,1792]{1,0:T(8,128)(2,1)S(1)}, u32[]{:S(2)}, u32[]{:S(2)}) %collective-permute-start.5) | collective-permute-done | bytes 688160 | tf_op jit(solution)/shard_map/ppermute | solution.py:167
  188.2 14.9 %collective-permute-done.3 = bf16[208,1792]{1,0:T(8,128)(2,1)S(1)} collective-permute-done((bf16[208,1792]{1,0:T(8,128)(2,1)}, bf16[208,1792]{1,0:T(8,128)(2,1)S(1)}, u32[]{:S(2)}, u32[]{:S(2)}) %collective-permute-start.3) | collective-permute-done | bytes 745504 | tf_op jit(solution)/shard_map/ppermute | solution.py:167
  203.1 7.9 %fusion.3 = (bf16[592,1792]{1,0:T(8,128)(2,1)S(1)}, f32[592,1792]{1,0:T(8,128)S(1)}, f32[592,1792]{1,0:T(8,128)S(1)}) fusion(bf16[192,1792]{1,0:T(8,128)(2,1)S(1)} %collective-permute-done.5, bf16[192,1792]{1,0:T(8,128)(2,1)S(1)} %collective-permute-done.4, bf16[208,1792]{1,0:T(8,128)(2,1)S(1)} %collective-permute-done.3, f32[]{:T(128)S(6)} %select_n.182, ...), kind=kOutput, calls=%fused_computation.15 | convolution fusion | flops 2193866752 | bytes 23977996 | tf_op jit(solution)/shard_map/dot_general | solution.py:202
  211.0 3.4 fusion.1
  214.7 3.8 %collective-permute-done.29 = bf16[512,1792]{1,0:T(8,128)(2,1)S(1)} collective-permute-done((bf16[512,1792]{1,0:T(8,128)(2,1)S(1)}, bf16[512,1792]{1,0:T(8,128)(2,1)S(1)}, u32[]{:S(2)}, u32[]{:S(2)}) %collective-permute-start.29) | collective-permute-done | bytes 1835040 | tf_op jit(solution)/shard_map/ppermute | solution.py:26
  219.0 3.2 collective-permute-start.31
  222.2 20.4 %collective-permute-done.30 = bf16[128,1792]{1,0:T(8,128)(2,1)S(1)} collective-permute-done((bf16[128,1792]{1,0:T(8,128)(2,1)S(1)}, bf16[128,1792]{1,0:T(8,128)(2,1)S(1)}, u32[]{:S(2)}, u32[]{:S(2)}) %collective-permute-start.30) | collective-permute-done | bytes 458784 | tf_op jit(solution)/shard_map/ppermute | solution.py:26
  242.9 1.1 collective-permute-start.33
  244.0 12.2 %collective-permute-done.33 = bf16[128,1792]{1,0:T(8,128)(2,1)S(1)} collective-permute-done((bf16[128,1792]{1,0:T(8,128)(2,1)S(1)}, bf16[128,1792]{1,0:T(8,128)(2,1)S(1)}, u32[]{:S(2)}, u32[]{:S(2)}) %collective-permute-start.33) | collective-permute-done | bytes 458784 | tf_op jit(solution)/shard_map/ppermute | solution.py:26
  256.6 2.7 collective-permute-start.34
  260.3 1.0 collective-permute-start.23
  261.3 16.0 %collective-permute-done.34 = bf16[128,1792]{1,0:T(8,128)(2,1)S(1)} collective-permute-done((bf16[128,1792]{1,0:T(8,128)(2,1)S(1)}, bf16[128,1792]{1,0:T(8,128)(2,1)S(1)}, u32[]{:S(2)}, u32[]{:S(2)}) %collective-permute-start.34) | collective-permute-done | bytes 458784 | tf_op jit(solution)/shard_map/ppermute | solution.py:26
  277.3 3.6 %collective-permute-done.36 = bf16[128,1792]{1,0:T(8,128)(2,1)S(1)} collective-permute-done((bf16[128,1792]{1,0:T(8,128)(2,1)S(1)}, bf16[128,1792]{1,0:T(8,128)(2,1)S(1)}, u32[]{:S(2)}, u32[]{:S(2)}) %collective-permute-start.36) | collective-permute-done | bytes 458784 | tf_op jit(solution)/shard_map/ppermute | solution.py:26
  281.2 1.0 collective-permute-start.24
  282.2 1.1 collective-permute-start.25
  283.3 16.3 %collective-permute-done.24 = bf16[192,1792]{1,0:T(8,128)(2,1)S(1)} collective-permute-done((bf16[192,1792]{1,0:T(8,128)(2,1)S(1)}, bf16[192,1792]{1,0:T(8,128)(2,1)S(1)}, u32[]{:S(2)}, u32[]{:S(2)}) %collective-permute-start.24) | collective-permute-done | bytes 688160 | tf_op jit(solution)/shard_map/ppermute | solution.py:166
  299.6 14.3 %collective-permute-done.25 = bf16[192,1792]{1,0:T(8,128)(2,1)S(1)} collective-permute-done((bf16[192,1792]{1,0:T(8,128)(2,1)S(1)}, bf16[192,1792]{1,0:T(8,128)(2,1)S(1)}, u32[]{:S(2)}, u32[]{:S(2)}) %collective-permute-start.25) | collective-permute-done | bytes 688160 | tf_op jit(solution)/shard_map/ppermute | solution.py:166
  313.9 1.5 collective-permute-start.26
  315.7 1.7 collective-permute-done.27
  317.4 16.0 %collective-permute-done.28 = bf16[192,1792]{1,0:T(8,128)(2,1)S(1)} collective-permute-done((bf16[192,1792]{1,0:T(8,128)(2,1)S(1)}, bf16[192,1792]{1,0:T(8,128)(2,1)S(1)}, u32[]{:S(2)}, u32[]{:S(2)}) %collective-permute-start.28) | collective-permute-done | bytes 688160 | tf_op jit(solution)/shard_map/ppermute | solution.py:167
  333.4 14.7 %collective-permute-done.26 = bf16[208,1792]{1,0:T(8,128)(2,1)S(1)} collective-permute-done((bf16[208,1792]{1,0:T(8,128)(2,1)S(1)}, bf16[208,1792]{1,0:T(8,128)(2,1)S(1)}, u32[]{:S(2)}, u32[]{:S(2)}) %collective-permute-start.26) | collective-permute-done | bytes 745504 | tf_op jit(solution)/shard_map/ppermute | solution.py:167
  348.1 5.2 %subtract_bitcast_fusion = f32[1,592,1792]{2,1,0:T(8,128)} fusion(f32[592,1792]{1,0:T(8,128)S(1)} %get-tuple-element.54, bf16[192,1792]{1,0:T(8,128)(2,1)S(1)} %collective-permute-done.25, bf16[192,1792]{1,0:T(8,128)(2,1)S(1)} %collective-permute-done.24, bf16[208,1792]{1,0:T(8,128)(2,1)S(1)} %collective-permute-done.23, ...), kind=kOutput, calls=%fused_computation.7 | convolution fusion | flops 2197049344 | bytes 21856268 | tf_op jit(solution)/shard_map/dot_general | solution.py:202
  (90 shorter events, 12.3 us)
Async XLA Ops:
  0.0 3.3 copy-start
  0.0 22.4 %copy-start.4 = (bf16[4096,112]{0,1:T(8,128)(2,1)S(1)}, bf16[4096,112]{0,1:T(8,128)(2,1)}, u32[]{:S(2)}) copy-start(bf16[4096,112]{0,1:T(8,128)(2,1)} %param.11) | copy-start | bytes 2752516
  8.4 26.8 %copy-start.3 = (bf16[112,1024]{1,0:T(8,128)(2,1)}, bf16[112,1024]{1,0:T(8,128)(2,1)S(1)}, u32[]{:S(2)}) copy-start(bf16[112,1024]{1,0:T(8,128)(2,1)S(1)} %select_bitcast_fusion.refs_0_) | copy-start | bytes 688132
  8.4 17.9 %collective-permute-start.10 = (bf16[112,1024]{1,0:T(8,128)(2,1)S(1)}, bf16[112,1024]{1,0:T(8,128)(2,1)S(1)}, u32[]{:S(2)}, u32[]{:S(2)}) collective-permute-start(bf16[112,1024]{1,0:T(8,128)(2,1)S(1)} %select_bitcast_fusion.refs_0_), channel_id=1, source_target_pairs={{0,12},{1,13},{2,14},{3,15},{4,8},{5,9},{6,10},{7,11},{8,4},{9,5},... | collective-permute-start | bytes 688136 | tf_op jit(solution)/shard_map/ppermute | solution.py:26
  14.3 15.5 %collective-permute-start.11 = (bf16[112,1024]{1,0:T(8,128)(2,1)S(1)}, bf16[112,1024]{1,0:T(8,128)(2,1)S(1)}, u32[]{:S(2)}, u32[]{:S(2)}) collective-permute-start(bf16[112,1024]{1,0:T(8,128)(2,1)S(1)} %select_bitcast_fusion.refs_0_), channel_id=1, source_target_pairs={{0,2},{1,3},{2,4},{3,5},{4,6},{5,7},{6,0},{7,1},{8,10},{9,11},{10,... | collective-permute-start | bytes 688136 | tf_op jit(solution)/shard_map/ppermute | solution.py:26
  15.0 20.3 %collective-permute-start.12 = (bf16[112,1024]{1,0:T(8,128)(2,1)S(1)}, bf16[112,1024]{1,0:T(8,128)(2,1)S(1)}, u32[]{:S(2)}, u32[]{:S(2)}) collective-permute-start(bf16[112,1024]{1,0:T(8,128)(2,1)S(1)} %select_bitcast_fusion.refs_0_), channel_id=1, source_target_pairs={{0,10},{1,11},{2,12},{3,13},{4,14},{5,15},{6,8},{7,9},{8,2},{9,3},... | collective-permute-start | bytes 688136 | tf_op jit(solution)/shard_map/ppermute | solution.py:26
  15.0 20.3 %collective-permute-start.6 = (bf16[112,1024]{1,0:T(8,128)(2,1)S(1)}, bf16[112,1024]{1,0:T(8,128)(2,1)S(1)}, u32[]{:S(2)}, u32[]{:S(2)}) collective-permute-start(bf16[112,1024]{1,0:T(8,128)(2,1)S(1)} %select_bitcast_fusion.refs_0_), channel_id=1, source_target_pairs={{0,8},{1,9},{2,10},{3,11},{4,12},{5,13},{6,14},{7,15},{8,0},{9,1},... | collective-permute-start | bytes 688136 | tf_op jit(solution)/shard_map/ppermute | solution.py:26
  17.9 17.3 %collective-permute-start.7 = (bf16[112,1024]{1,0:T(8,128)(2,1)S(1)}, bf16[112,1024]{1,0:T(8,128)(2,1)}, u32[]{:S(2)}, u32[]{:S(2)}) collective-permute-start(bf16[112,1024]{1,0:T(8,128)(2,1)S(1)} %select_bitcast_fusion.refs_0_), channel_id=1, source_target_pairs={{0,6},{1,7},{2,0},{3,1},{4,2},{5,3},{6,4},{7,5},{8,14},{9,15},{10,... | collective-permute-start | bytes 688136 | tf_op jit(solution)/shard_map/ppermute | solution.py:26
  26.4 12.4 %copy-start.5 = (bf16[112,1024]{1,0:T(8,128)(2,1)}, bf16[112,1024]{1,0:T(8,128)(2,1)S(1)}, u32[]{:S(2)}) copy-start(bf16[112,1024]{1,0:T(8,128)(2,1)S(1)} %collective-permute-done.10.refs_5_) | copy-start | bytes 688132
  26.4 9.3 %collective-permute-start.8 = (bf16[112,1024]{1,0:T(8,128)(2,1)S(1)}, bf16[112,1024]{1,0:T(8,128)(2,1)S(1)}, u32[]{:S(2)}, u32[]{:S(2)}) collective-permute-start(bf16[112,1024]{1,0:T(8,128)(2,1)S(1)} %select_bitcast_fusion.refs_0_), channel_id=1, source_target_pairs={{0,14},{1,15},{2,8},{3,9},{4,10},{5,11},{6,12},{7,13},{8,6},{9,7},... | collective-permute-start | bytes 688136 | tf_op jit(solution)/shard_map/ppermute | solution.py:26
  29.8 9.0 %copy-start.6 = (bf16[112,1024]{1,0:T(8,128)(2,1)}, bf16[112,1024]{1,0:T(8,128)(2,1)S(1)}, u32[]{:S(2)}) copy-start(bf16[112,1024]{1,0:T(8,128)(2,1)S(1)} %collective-permute-done.11.refs_6_) | copy-start | bytes 688132
  29.8 9.0 %collective-permute-start.9 = (bf16[112,1024]{1,0:T(8,128)(2,1)S(1)}, bf16[112,1024]{1,0:T(8,128)(2,1)S(1)}, u32[]{:S(2)}, u32[]{:S(2)}) collective-permute-start(bf16[112,1024]{1,0:T(8,128)(2,1)S(1)} %select_bitcast_fusion.refs_0_), channel_id=1, source_target_pairs={{0,4},{1,5},{2,6},{3,7},{4,0},{5,1},{6,2},{7,3},{8,12},{9,13},{10,... | collective-permute-start | bytes 688136 | tf_op jit(solution)/shard_map/ppermute | solution.py:26
  35.2 3.6 %copy-start.7 = (bf16[112,1024]{1,0:T(8,128)(2,1)}, bf16[112,1024]{1,0:T(8,128)(2,1)S(1)}, u32[]{:S(2)}) copy-start(bf16[112,1024]{1,0:T(8,128)(2,1)S(1)} %collective-permute-done.12.refs_7_) | copy-start | bytes 688132
  35.2 3.6 %copy-start.8 = (bf16[112,1024]{1,0:T(8,128)(2,1)}, bf16[112,1024]{1,0:T(8,128)(2,1)S(1)}, u32[]{:S(2)}) copy-start(bf16[112,1024]{1,0:T(8,128)(2,1)S(1)} %collective-permute-done.6.refs_1_) | copy-start | bytes 688132
  35.7 3.1 copy-start.9
  38.8 0.7 copy-start.10
  42.2 4.1 %collective-permute-start.13 = (bf16[896,1024]{1,0:T(8,128)(2,1)}, bf16[896,1024]{1,0:T(8,128)(2,1)}, u32[]{:S(2)}, u32[]{:S(2)}) collective-permute-start(bf16[896,1024]{1,0:T(8,128)(2,1)} %stack.1.plane_ref), channel_id=1, source_target_pairs={{0,1},{1,0},{2,3},{3,2},{4,5},{5,4},{6,7},{7,6},{8,9},{9,8},{10,11... | collective-permute-start | bytes 5505032 | tf_op jit(solution)/shard_map/ppermute | solution.py:26
  63.2 3.9 %collective-permute-start.14 = (bf16[512,1792]{1,0:T(8,128)(2,1)S(1)}, bf16[512,1792]{1,0:T(8,128)(2,1)S(1)}, u32[]{:S(2)}, u32[]{:S(2)}) collective-permute-start(bf16[512,1792]{1,0:T(8,128)(2,1)S(1)} %slice.98), channel_id=1, source_target_pairs={{0,1},{1,0},{2,3},{3,2},{4,5},{5,4},{6,7},{7,6},{8,9},{9,8},{10,11... | collective-permute-start | bytes 5505032 | tf_op jit(solution)/shard_map/ppermute | solution.py:26
  67.6 15.3 %collective-permute-start.15 = (bf16[128,1792]{1,0:T(8,128)(2,1)S(1)}, bf16[128,1792]{1,0:T(8,128)(2,1)S(1)}, u32[]{:S(2)}, u32[]{:S(2)}) collective-permute-start(bf16[128,1792]{1,0:T(8,128)(2,1)S(1)} %get-tuple-element.51), channel_id=1, source_target_pairs={{0,2},{1,3},{2,4},{3,5},{4,6},{5,7},{6,0},{7,1},{8,10},{9,11},{10,... | collective-permute-start | bytes 1376264 | tf_op jit(solution)/shard_map/ppermute | solution.py:26
  69.9 22.1 %collective-permute-start.16 = (bf16[128,1792]{1,0:T(8,128)(2,1)S(1)}, bf16[128,1792]{1,0:T(8,128)(2,1)S(1)}, u32[]{:S(2)}, u32[]{:S(2)}) collective-permute-start(bf16[128,1792]{1,0:T(8,128)(2,1)S(1)} %get-tuple-element.53), channel_id=1, source_target_pairs={{0,6},{1,7},{2,0},{3,1},{4,2},{5,3},{6,4},{7,5},{8,14},{9,15},{10,... | collective-permute-start | bytes 1376264 | tf_op jit(solution)/shard_map/ppermute | solution.py:26
  72.1 21.7 %collective-permute-start.17 = (bf16[128,1792]{1,0:T(8,128)(2,1)S(1)}, bf16[128,1792]{1,0:T(8,128)(2,1)S(1)}, u32[]{:S(2)}, u32[]{:S(2)}) collective-permute-start(bf16[128,1792]{1,0:T(8,128)(2,1)S(1)} %get-tuple-element.52), channel_id=1, source_target_pairs={{0,4},{1,5},{2,6},{3,7},{4,0},{5,1},{6,2},{7,3},{8,12},{9,13},{10,... | collective-permute-start | bytes 1376264 | tf_op jit(solution)/shard_map/ppermute | solution.py:26
  94.2 13.3 %collective-permute-start.18 = (bf16[128,1792]{1,0:T(8,128)(2,1)S(1)}, bf16[128,1792]{1,0:T(8,128)(2,1)S(1)}, u32[]{:S(2)}, u32[]{:S(2)}) collective-permute-start(bf16[128,1792]{1,0:T(8,128)(2,1)S(1)} %fusion.39), channel_id=1, source_target_pairs={{0,8},{1,9},{2,10},{3,11},{4,12},{5,13},{6,14},{7,15},{8,0},{9,1},... | collective-permute-start | bytes 1376264 | tf_op jit(solution)/shard_map/ppermute | solution.py:26
  108.6 28.4 %copy-start.11 = (f32[8]{0:T(128)S(1)}, f32[8]{0:T(128)}, u32[]{:S(2)}) copy-start(f32[8]{0:T(128)} %param.17) | copy-start | bytes 100
  108.6 20.1 %collective-permute-start.19 = (bf16[128,1792]{1,0:T(8,128)(2,1)S(1)}, bf16[128,1792]{1,0:T(8,128)(2,1)S(1)}, u32[]{:S(2)}, u32[]{:S(2)}) collective-permute-start(bf16[128,1792]{1,0:T(8,128)(2,1)S(1)} %get-tuple-element.41), channel_id=1, source_target_pairs={{0,6},{1,7},{2,0},{3,1},{4,2},{5,3},{6,4},{7,5},{8,14},{9,15},{10,... | collective-permute-start | bytes 1376264 | tf_op jit(solution)/shard_map/ppermute | solution.py:26
  110.5 18.2 %collective-permute-start.20 = (bf16[128,1792]{1,0:T(8,128)(2,1)S(1)}, bf16[128,1792]{1,0:T(8,128)(2,1)S(1)}, u32[]{:S(2)}, u32[]{:S(2)}) collective-permute-start(bf16[128,1792]{1,0:T(8,128)(2,1)S(1)} %get-tuple-element.41), channel_id=1, source_target_pairs={{0,4},{1,5},{2,6},{3,7},{4,0},{5,1},{6,2},{7,3},{8,12},{9,13},{10,... | collective-permute-start | bytes 1376264 | tf_op jit(solution)/shard_map/ppermute | solution.py:26
  111.6 20.8 %collective-permute-start.21 = (bf16[128,1792]{1,0:T(8,128)(2,1)S(1)}, bf16[128,1792]{1,0:T(8,128)(2,1)S(1)}, u32[]{:S(2)}, u32[]{:S(2)}) collective-permute-start(bf16[128,1792]{1,0:T(8,128)(2,1)S(1)} %get-tuple-element.41), channel_id=1, source_target_pairs={{0,2},{1,3},{2,4},{3,5},{4,6},{5,7},{6,0},{7,1},{8,10},{9,11},{10,... | collective-permute-start | bytes 1376264 | tf_op jit(solution)/shard_map/ppermute | solution.py:26
  112.5 57.3 %collective-permute-start = (bf16[208,1792]{1,0:T(8,128)(2,1)}, bf16[208,1792]{1,0:T(8,128)(2,1)}, u32[]{:S(2)}, u32[]{:S(2)}) collective-permute-start(bf16[208,1792]{1,0:T(8,128)(2,1)} %slice.94), channel_id=1, source_target_pairs={{0,16},{16,0},{32,48},{48,32},{64,80},{80,64},{96,112},{112,96},{1... | collective-permute-start | bytes 2236424 | tf_op jit(solution)/shard_map/ppermute | solution.py:166
  133.8 40.4 %collective-permute-start.22 = (bf16[512,1792]{1,0:T(8,128)(2,1)}, bf16[512,1792]{1,0:T(8,128)(2,1)}, u32[]{:S(2)}, u32[]{:S(2)}) collective-permute-start(bf16[512,1792]{1,0:T(8,128)(2,1)} %pad_maximum_fusion), channel_id=1, source_target_pairs={{0,1},{1,0},{2,3},{3,2},{4,5},{5,4},{6,7},{7,6},{8,9},{9,8},{10,11... | collective-permute-start | bytes 5505032 | tf_op jit(solution)/shard_map/ppermute | solution.py:26
  135.0 18.5 %collective-permute-start.1 = (bf16[192,1792]{1,0:T(8,128)(2,1)}, bf16[192,1792]{1,0:T(8,128)(2,1)S(1)}, u32[]{:S(2)}, u32[]{:S(2)}) collective-permute-start(bf16[192,1792]{1,0:T(8,128)(2,1)} %get-tuple-element.46), channel_id=1, source_target_pairs={{0,16},{16,0},{32,48},{48,32},{64,80},{80,64},{96,112},{112,96},{1... | collective-permute-start | bytes 2064392 | tf_op jit(solution)/shard_map/ppermute | solution.py:166
  136.6 31.3 %collective-permute-start.2 = (bf16[192,1792]{1,0:T(8,128)(2,1)}, bf16[192,1792]{1,0:T(8,128)(2,1)S(1)}, u32[]{:S(2)}, u32[]{:S(2)}) collective-permute-start(bf16[192,1792]{1,0:T(8,128)(2,1)} %get-tuple-element.47), channel_id=1, source_target_pairs={{0,16},{16,0},{32,48},{48,32},{64,80},{80,64},{96,112},{112,96},{1... | collective-permute-start | bytes 2064392 | tf_op jit(solution)/shard_map/ppermute | solution.py:166
  141.1 62.0 %copy-start.12 = (bf16[592,1024]{1,0:T(8,128)(2,1)S(1)}, bf16[592,1024]{1,0:T(8,128)(2,1)}, u32[]{:S(2)}) copy-start(bf16[592,1024]{1,0:T(8,128)(2,1)} %get-tuple-element.31) | copy-start | bytes 3637252
  153.6 23.4 %collective-permute-start.4 = (bf16[192,1792]{1,0:T(8,128)(2,1)S(1)}, bf16[192,1792]{1,0:T(8,128)(2,1)S(1)}, u32[]{:S(2)}, u32[]{:S(2)}) collective-permute-start(bf16[192,1792]{1,0:T(8,128)(2,1)S(1)} %collective-permute-done.1), channel_id=1, source_target_pairs={{0,32},{16,112},{32,64},{48,16},{64,96},{80,48},{96,0},{112,80},{1... | collective-permute-start | bytes 2064392 | tf_op jit(solution)/shard_map/ppermute | solution.py:167
  167.8 20.3 %collective-permute-start.5 = (bf16[192,1792]{1,0:T(8,128)(2,1)S(1)}, bf16[192,1792]{1,0:T(8,128)(2,1)S(1)}, u32[]{:S(2)}, u32[]{:S(2)}) collective-permute-start(bf16[192,1792]{1,0:T(8,128)(2,1)S(1)} %collective-permute-done.2), channel_id=1, source_target_pairs={{0,32},{16,112},{32,64},{48,16},{64,96},{80,48},{96,0},{112,80},{1... | collective-permute-start | bytes 2064392 | tf_op jit(solution)/shard_map/ppermute | solution.py:167
  169.8 33.3 %collective-permute-start.3 = (bf16[208,1792]{1,0:T(8,128)(2,1)}, bf16[208,1792]{1,0:T(8,128)(2,1)S(1)}, u32[]{:S(2)}, u32[]{:S(2)}) collective-permute-start(bf16[208,1792]{1,0:T(8,128)(2,1)} %collective-permute-done), channel_id=1, source_target_pairs={{0,32},{16,112},{32,64},{48,16},{64,96},{80,48},{96,0},{112,80},{1... | collective-permute-start | bytes 2236424 | tf_op jit(solution)/shard_map/ppermute | solution.py:167
  203.1 7.9 %copy-start.2 = (bf16[1024,1792]{1,0:T(8,128)(2,1)S(1)}, bf16[1024,1792]{1,0:T(8,128)(2,1)}, u32[]{:S(2)}) copy-start(bf16[1024,1792]{1,0:T(8,128)(2,1)} %convolution_convert_fusion) | copy-start | bytes 11010052
  203.1 7.9 %copy-start.13 = (bf16[1024,592]{1,0:T(8,128)(2,1)S(1)}, bf16[1024,592]{1,0:T(8,128)(2,1)}, u32[]{:S(2)}) copy-start(bf16[1024,592]{1,0:T(8,128)(2,1)} %get-tuple-element.32) | copy-start | bytes 3637252
  214.6 3.9 %collective-permute-start.29 = (bf16[512,1792]{1,0:T(8,128)(2,1)S(1)}, bf16[512,1792]{1,0:T(8,128)(2,1)S(1)}, u32[]{:S(2)}, u32[]{:S(2)}) collective-permute-start(bf16[512,1792]{1,0:T(8,128)(2,1)S(1)} %slice.109), channel_id=1, source_target_pairs={{0,1},{1,0},{2,3},{3,2},{4,5},{5,4},{6,7},{7,6},{8,9},{9,8},{10,11... | collective-permute-start | bytes 5505032 | tf_op jit(solution)/shard_map/ppermute | solution.py:26
  218.9 23.7 %collective-permute-start.30 = (bf16[128,1792]{1,0:T(8,128)(2,1)S(1)}, bf16[128,1792]{1,0:T(8,128)(2,1)S(1)}, u32[]{:S(2)}, u32[]{:S(2)}) collective-permute-start(bf16[128,1792]{1,0:T(8,128)(2,1)S(1)} %get-tuple-element.48), channel_id=1, source_target_pairs={{0,2},{1,3},{2,4},{3,5},{4,6},{5,7},{6,0},{7,1},{8,10},{9,11},{10,... | collective-permute-start | bytes 1376264 | tf_op jit(solution)/shard_map/ppermute | solution.py:26
  219.0 23.6 %collective-permute-start.31 = (bf16[128,1792]{1,0:T(8,128)(2,1)S(1)}, bf16[128,1792]{1,0:T(8,128)(2,1)S(1)}, u32[]{:S(2)}, u32[]{:S(2)}) collective-permute-start(bf16[128,1792]{1,0:T(8,128)(2,1)S(1)} %get-tuple-element.50), channel_id=1, source_target_pairs={{0,6},{1,7},{2,0},{3,1},{4,2},{5,3},{6,4},{7,5},{8,14},{9,15},{10,... | collective-permute-start | bytes 1376264 | tf_op jit(solution)/shard_map/ppermute | solution.py:26
  222.2 20.4 %collective-permute-start.32 = (bf16[128,1792]{1,0:T(8,128)(2,1)S(1)}, bf16[128,1792]{1,0:T(8,128)(2,1)S(1)}, u32[]{:S(2)}, u32[]{:S(2)}) collective-permute-start(bf16[128,1792]{1,0:T(8,128)(2,1)S(1)} %get-tuple-element.49), channel_id=1, source_target_pairs={{0,4},{1,5},{2,6},{3,7},{4,0},{5,1},{6,2},{7,3},{8,12},{9,13},{10,... | collective-permute-start | bytes 1376264 | tf_op jit(solution)/shard_map/ppermute | solution.py:26
  242.9 13.3 %collective-permute-start.33 = (bf16[128,1792]{1,0:T(8,128)(2,1)S(1)}, bf16[128,1792]{1,0:T(8,128)(2,1)S(1)}, u32[]{:S(2)}, u32[]{:S(2)}) collective-permute-start(bf16[128,1792]{1,0:T(8,128)(2,1)S(1)} %fusion.40), channel_id=1, source_target_pairs={{0,8},{1,9},{2,10},{3,11},{4,12},{5,13},{6,14},{7,15},{8,0},{9,1},... | collective-permute-start | bytes 1376264 | tf_op jit(solution)/shard_map/ppermute | solution.py:26
  256.6 20.7 %collective-permute-start.34 = (bf16[128,1792]{1,0:T(8,128)(2,1)S(1)}, bf16[128,1792]{1,0:T(8,128)(2,1)S(1)}, u32[]{:S(2)}, u32[]{:S(2)}) collective-permute-start(bf16[128,1792]{1,0:T(8,128)(2,1)S(1)} %get-tuple-element.39), channel_id=1, source_target_pairs={{0,6},{1,7},{2,0},{3,1},{4,2},{5,3},{6,4},{7,5},{8,14},{9,15},{10,... | collective-permute-start | bytes 1376264 | tf_op jit(solution)/shard_map/ppermute | solution.py:26
  259.3 18.0 %collective-permute-start.35 = (bf16[128,1792]{1,0:T(8,128)(2,1)S(1)}, bf16[128,1792]{1,0:T(8,128)(2,1)S(1)}, u32[]{:S(2)}, u32[]{:S(2)}) collective-permute-start(bf16[128,1792]{1,0:T(8,128)(2,1)S(1)} %get-tuple-element.39), channel_id=1, source_target_pairs={{0,4},{1,5},{2,6},{3,7},{4,0},{5,1},{6,2},{7,3},{8,12},{9,13},{10,... | collective-permute-start | bytes 1376264 | tf_op jit(solution)/shard_map/ppermute | solution.py:26
  259.6 21.3 %collective-permute-start.36 = (bf16[128,1792]{1,0:T(8,128)(2,1)S(1)}, bf16[128,1792]{1,0:T(8,128)(2,1)S(1)}, u32[]{:S(2)}, u32[]{:S(2)}) collective-permute-start(bf16[128,1792]{1,0:T(8,128)(2,1)S(1)} %get-tuple-element.39), channel_id=1, source_target_pairs={{0,2},{1,3},{2,4},{3,5},{4,6},{5,7},{6,0},{7,1},{8,10},{9,11},{10,... | collective-permute-start | bytes 1376264 | tf_op jit(solution)/shard_map/ppermute | solution.py:26
  260.3 53.6 %collective-permute-start.23 = (bf16[208,1792]{1,0:T(8,128)(2,1)S(1)}, bf16[208,1792]{1,0:T(8,128)(2,1)S(1)}, u32[]{:S(2)}, u32[]{:S(2)}) collective-permute-start(bf16[208,1792]{1,0:T(8,128)(2,1)S(1)} %slice.105), channel_id=1, source_target_pairs={{0,16},{16,0},{32,48},{48,32},{64,80},{80,64},{96,112},{112,96},{1... | collective-permute-start | bytes 2236424 | tf_op jit(solution)/shard_map/ppermute | solution.py:166
  281.0 34.5 %collective-permute-start.37 = (bf16[512,1792]{1,0:T(8,128)(2,1)S(1)}, bf16[512,1792]{1,0:T(8,128)(2,1)S(1)}, u32[]{:S(2)}, u32[]{:S(2)}) collective-permute-start(bf16[512,1792]{1,0:T(8,128)(2,1)S(1)} %pad_maximum_fusion.1), channel_id=1, source_target_pairs={{0,1},{1,0},{2,3},{3,2},{4,5},{5,4},{6,7},{7,6},{8,9},{9,8},{10,11... | collective-permute-start | bytes 5505032 | tf_op jit(solution)/shard_map/ppermute | solution.py:26
  281.2 18.4 %collective-permute-start.24 = (bf16[192,1792]{1,0:T(8,128)(2,1)S(1)}, bf16[192,1792]{1,0:T(8,128)(2,1)S(1)}, u32[]{:S(2)}, u32[]{:S(2)}) collective-permute-start(bf16[192,1792]{1,0:T(8,128)(2,1)S(1)} %get-tuple-element.44), channel_id=1, source_target_pairs={{0,16},{16,0},{32,48},{48,32},{64,80},{80,64},{96,112},{112,96},{1... | collective-permute-start | bytes 2064392 | tf_op jit(solution)/shard_map/ppermute | solution.py:166
  282.2 31.7 %collective-permute-start.25 = (bf16[192,1792]{1,0:T(8,128)(2,1)S(1)}, bf16[192,1792]{1,0:T(8,128)(2,1)S(1)}, u32[]{:S(2)}, u32[]{:S(2)}) collective-permute-start(bf16[192,1792]{1,0:T(8,128)(2,1)S(1)} %get-tuple-element.45), channel_id=1, source_target_pairs={{0,16},{16,0},{32,48},{48,32},{64,80},{80,64},{96,112},{112,96},{1... | collective-permute-start | bytes 2064392 | tf_op jit(solution)/shard_map/ppermute | solution.py:166
  299.6 17.8 %collective-permute-start.27 = (bf16[192,1792]{1,0:T(8,128)(2,1)S(1)}, bf16[192,1792]{1,0:T(8,128)(2,1)S(1)}, u32[]{:S(2)}, u32[]{:S(2)}) collective-permute-start(bf16[192,1792]{1,0:T(8,128)(2,1)S(1)} %collective-permute-done.24), channel_id=1, source_target_pairs={{0,32},{16,112},{32,64},{48,16},{64,96},{80,48},{96,0},{112,80},{1... | collective-permute-start | bytes 2064392 | tf_op jit(solution)/shard_map/ppermute | solution.py:167
  313.9 19.5 %collective-permute-start.28 = (bf16[192,1792]{1,0:T(8,128)(2,1)S(1)}, bf16[192,1792]{1,0:T(8,128)(2,1)S(1)}, u32[]{:S(2)}, u32[]{:S(2)}) collective-permute-start(bf16[192,1792]{1,0:T(8,128)(2,1)S(1)} %collective-permute-done.25), channel_id=1, source_target_pairs={{0,32},{16,112},{32,64},{48,16},{64,96},{80,48},{96,0},{112,80},{1... | collective-permute-start | bytes 2064392 | tf_op jit(solution)/shard_map/ppermute | solution.py:167
  313.9 34.2 %collective-permute-start.26 = (bf16[208,1792]{1,0:T(8,128)(2,1)S(1)}, bf16[208,1792]{1,0:T(8,128)(2,1)S(1)}, u32[]{:S(2)}, u32[]{:S(2)}) collective-permute-start(bf16[208,1792]{1,0:T(8,128)(2,1)S(1)} %collective-permute-done.23), channel_id=1, source_target_pairs={{0,32},{16,112},{32,64},{48,16},{64,96},{80,48},{96,0},{112,80},{1... | collective-permute-start | bytes 2236424 | tf_op jit(solution)/shard_map/ppermute | solution.py:167
  348.1 5.2 %copy-start.1 = (s32[8,1024]{1,0:T(8,128)S(1)}, s32[8,1024]{1,0:T(8,128)}, u32[]{:S(2)}) copy-start(s32[8,1024]{1,0:T(8,128)} %param.15) | copy-start | bytes 98308
